TPU v7x, 32 devices: a whole 2x2x4 slice. The times are simulated.
32 devices in a mesh: fsdp: 8 (over y, x, core), tp: 4 (over z).
Axes of the slice: x: 2, y: 2, z: 4, core: 2. Of those that a mesh axis runs over, the one named last changes fastest.
Arguments:
- tokens: bfloat16 [8192, 1024], P(('fsdp', 'tp')), may hold values from -6 to 6
- lengths: int32 [8], P('fsdp'), may hold values from 1024 to 1024, as said below
- gain_mix: bfloat16 [1024], P(('tp', 'fsdp')), may hold values from 0.25 to 1.75
- w_query: bfloat16 [1024, 1024], P('fsdp', 'tp'), may hold values from -0.1875 to 0.1875
- w_key: bfloat16 [1024, 1024], P('fsdp', 'tp'), may hold values from -0.1875 to 0.1875
- w_value: bfloat16 [1024, 2048], P('fsdp', 'tp'), may hold values from -0.1875 to 0.1875
- w_outgate: bfloat16 [1024, 2048], P('fsdp', 'tp'), may hold values from -0.1875 to 0.1875
- w_beta: bfloat16 [1024, 8], P('fsdp', 'tp'), may hold values from -0.1875 to 0.1875
- w_decay: bfloat16 [1024, 8], P('fsdp', 'tp'), may hold values from -0.1875 to 0.1875
- conv_query: bfloat16 [4, 1024], P(None, ('tp', 'fsdp')), may hold values from -3 to 3
- conv_key: bfloat16 [4, 1024], P(None, ('tp', 'fsdp')), may hold values from -3 to 3
- conv_value: bfloat16 [4, 2048], P(None, ('tp', 'fsdp')), may hold values from -3 to 3
- decay_log: bfloat16 [8], P('tp'), may hold values from 0 to 2.6875
- decay_bias: bfloat16 [8], P('tp'), may hold values from -6.875 to -2.296875
- gain_head: bfloat16 [256], P(('tp', 'fsdp')), may hold values from 0.25 to 1.75
- w_out: bfloat16 [2048, 1024], P('tp', 'fsdp'), may hold values from -0.25 to 0.25
- gain_ff: bfloat16 [1024], P(('tp', 'fsdp')), may hold values from 0.25 to 1.75
- w_gate: bfloat16 [1024, 2816], P('fsdp', 'tp'), may hold values from -0.1875 to 0.1875
- w_up: bfloat16 [1024, 2816], P('fsdp', 'tp'), may hold values from -0.1875 to 0.1875
- w_down: bfloat16 [2816, 1024], P('tp', 'fsdp'), may hold values from -0.109375 to 0.109375
- cotangent: bfloat16 [8192, 1024], P(('fsdp', 'tp')), may hold values from -6 to 6
Outputs:
- layer_out: bfloat16 [8192, 1024], P(('fsdp', 'tp'))
- input_grad: float32 [8192, 1024], P(('fsdp', 'tp'))
- gain_mix_grad: float32 [1024], P(('tp', 'fsdp'))
- w_query_grad: float32 [1024, 1024], P('fsdp', 'tp')
- w_key_grad: float32 [1024, 1024], P('fsdp', 'tp')
- w_value_grad: float32 [1024, 2048], P('fsdp', 'tp')
- w_outgate_grad: float32 [1024, 2048], P('fsdp', 'tp')
- w_beta_grad: float32 [1024, 8], P('fsdp', 'tp')
- w_decay_grad: float32 [1024, 8], P('fsdp', 'tp')
- conv_query_grad: float32 [4, 1024], P(None, ('tp', 'fsdp'))
- conv_key_grad: float32 [4, 1024], P(None, ('tp', 'fsdp'))
- conv_value_grad: float32 [4, 2048], P(None, ('tp', 'fsdp'))
- decay_log_grad: float32 [8], P('tp')
- decay_bias_grad: float32 [8], P('tp')
- gain_head_grad: float32 [256], P(('tp', 'fsdp'))
- w_out_grad: float32 [2048, 1024], P('tp', 'fsdp')
- gain_ff_grad: float32 [1024], P(('tp', 'fsdp'))
- w_gate_grad: float32 [1024, 2816], P('fsdp', 'tp')
- w_up_grad: float32 [1024, 2816], P('fsdp', 'tp')
- w_down_grad: float32 [2816, 1024], P('tp', 'fsdp')
Inputs may be any that keep to these rules, and one draw needn't show every extreme that they name: lengths[g] is how many leading slots of group g hold its sequence; the other slots are padding; at least one group is full.
All inputs are finite; a program needn't handle non-finite values.
Results may differ from a plain program's by a relative error of at most 0.025.
Values may be sent and summed in bfloat16 or wider, within the bound.
A program may use at most 256 MiB of HBM per device.

v0:
```python
import jax
import jax.numpy as jnp
from jax import lax
from jax.sharding import PartitionSpec as P

SPAN = 64


epsilon = 1e-06


def batched(left, right):
    return jnp.einsum("...ij,...jk->...ik", left, right, precision=lax.Precision.HIGHEST)


def norm_scale(values):
    return lax.rsqrt(jnp.mean(values * values, axis=-1, keepdims=True) + epsilon)


def causal_conv(signal, kernel_taps):
    tap_count = kernel_taps.shape[0]
    length = signal.shape[0]
    padded = jnp.concatenate(
        [jnp.zeros((tap_count - 1, signal.shape[1]), jnp.float32), signal], axis=0
    )
    summed = kernel_taps[0] * signal
    for offset in range(1, tap_count):
        summed = (
            summed
            + kernel_taps[offset] * padded[tap_count - 1 - offset : tap_count - 1 - offset + length]
        )
    return summed


def prepare(
    query_proj,
    key_proj,
    value_proj,
    beta_logit,
    decay_logit,
    conv_query,
    conv_key,
    conv_value,
    decay_log,
    decay_bias,
):
    row_count = query_proj.shape[0]
    head_count = beta_logit.shape[1]
    queries = jax.nn.silu(causal_conv(query_proj, conv_query)).reshape(row_count, head_count, -1)
    keys_raw = jax.nn.silu(causal_conv(key_proj, conv_key)).reshape(row_count, head_count, -1)
    value_rows = jax.nn.silu(causal_conv(value_proj, conv_value)).reshape(row_count, head_count, -1)
    query_rows = (
        queries
        * lax.rsqrt(jnp.sum(queries * queries, axis=-1, keepdims=True) + epsilon)
        * queries.shape[-1] ** (-0.5)
    )
    key_rows = keys_raw * lax.rsqrt(jnp.sum(keys_raw * keys_raw, axis=-1, keepdims=True) + epsilon)
    beta_rows = jax.nn.sigmoid(beta_logit)
    decay_rows = -jnp.exp(decay_log) * jax.nn.softplus(decay_logit + decay_bias)
    return (query_rows, key_rows, value_rows, beta_rows, decay_rows)


def span_inverse(system):
    size = system.shape[-1]
    result = jnp.eye(size, dtype=jnp.float32) - system
    power = batched(system, system)
    levels = size.bit_length() - 2
    for level in range(levels):
        result = result + batched(result, power)
        if level + 1 < levels:
            power = batched(power, power)
    return result


def delta_rule(query_rows, key_rows, value_rows, beta_rows, decay_rows, block_size):
    row_count, head_count, key_size = query_rows.shape
    value_size = value_rows.shape[-1]
    blocks = row_count // block_size

    def split(values):
        return values.reshape((blocks, block_size) + values.shape[1:])

    queries, keys_all, values_all = (split(query_rows), split(key_rows), split(value_rows))
    betas, decays = (split(beta_rows), split(decay_rows))
    cumulative = jnp.cumsum(decays, axis=1)
    cum_heads = jnp.transpose(cumulative, (0, 2, 1))
    betas_heads = jnp.transpose(betas, (0, 2, 1))
    index = jnp.arange(block_size)
    strict = (index[:, None] > index[None, :])[None, None]
    within = (index[:, None] >= index[None, :])[None, None]
    spread = cum_heads[:, :, :, None] - cum_heads[:, :, None, :]
    strict_decay = jnp.where(strict, jnp.exp(jnp.where(strict, spread, 0.0)), 0.0)
    within_decay = jnp.where(within, jnp.exp(jnp.where(within, spread, 0.0)), 0.0)
    key_gram = jnp.einsum("nihd,njhd->nhij", keys_all, keys_all, precision=lax.Precision.HIGHEST)
    system = betas_heads[:, :, :, None] * strict_decay * key_gram
    inverse = span_inverse(system)
    growth = jnp.exp(cumulative)
    weighted_keys = jnp.einsum(
        "nhij,njhd->nhid",
        inverse,
        keys_all * (betas * growth)[..., None],
        precision=lax.Precision.HIGHEST,
    )
    weighted_values = jnp.einsum(
        "nhij,njhv->nhiv", inverse, values_all * betas[..., None], precision=lax.Precision.HIGHEST
    )
    scores = within_decay * jnp.einsum(
        "nihd,njhd->nhij", queries, keys_all, precision=lax.Precision.HIGHEST
    )
    scaled_queries = queries * growth[..., None]
    last_sum = cum_heads[:, :, -1]
    tails = jnp.exp(last_sum[:, :, None] - cum_heads)

    def advance(state, block_data):
        w_keys, w_values, block_scores, s_queries, block_keys, block_tail, block_last = block_data
        update = w_values - jnp.einsum(
            "hid,hvd->hiv", w_keys, state, precision=lax.Precision.HIGHEST
        )
        output = jnp.einsum("ihd,hvd->ihv", s_queries, state, precision=lax.Precision.HIGHEST)
        output = output + jnp.einsum(
            "hij,hjv->ihv", block_scores, update, precision=lax.Precision.HIGHEST
        )
        state = jnp.exp(block_last)[:, None, None] * state + jnp.einsum(
            "hjv,jhd->hvd",
            update * block_tail[..., None],
            block_keys,
            precision=lax.Precision.HIGHEST,
        )
        return (state, output)

    initial = jnp.zeros((head_count, value_size, key_size), jnp.float32)
    final_state, outputs = lax.scan(
        jax.checkpoint(advance),
        initial,
        (weighted_keys, weighted_values, scores, scaled_queries, keys_all, tails, last_sum),
    )
    return outputs.reshape(row_count, head_count, value_size)


def run_delta(query_rows, key_rows, value_rows, beta_rows, decay_rows):
    return delta_rule(query_rows, key_rows, value_rows, beta_rows, decay_rows, SPAN)


def finish(mixed, gate_proj, gain_head):
    row_count, head_count, value_size = mixed.shape
    normed = mixed * norm_scale(mixed) * gain_head
    gated = normed * jax.nn.silu(gate_proj.reshape(row_count, head_count, value_size))
    return gated.reshape(row_count, head_count * value_size)


def round_trip(values):
    return lax.optimization_barrier(values.astype(jnp.bfloat16)).astype(jnp.float32)


def norm_back(grad_normed, values, scale, gain):
    unit = values * scale
    gain_grad = jnp.sum(grad_normed * unit, axis=0)
    pulled = grad_normed * gain
    input_part = scale * (pulled - unit * jnp.mean(pulled * unit, axis=-1, keepdims=True))
    return (input_part, gain_grad)


def body(
    tokens,
    lengths,
    gain_mix,
    w_query,
    w_key,
    w_value,
    w_outgate,
    w_beta,
    w_decay,
    conv_query,
    conv_key,
    conv_value,
    decay_log,
    decay_bias,
    gain_head,
    w_out,
    gain_ff,
    w_gate,
    w_up,
    w_down,
    cotangent,
):
    contract_cols = (((1,), (1,)), ((), ()))
    contract_rows = (((0,), (0,)), ((), ()))
    (
        query_full,
        key_full,
        value_full,
        outgate_full,
        beta_full,
        decay_full,
        convq_full,
        convk_full,
        convv_full,
        mix_gain_part,
        head_gain_part,
        out_full,
    ) = (
        lax.all_gather(w_query, "fsdp", axis=0, tiled=True),
        lax.all_gather(w_key, "fsdp", axis=0, tiled=True),
        lax.all_gather(w_value, "fsdp", axis=0, tiled=True),
        lax.all_gather(w_outgate, "fsdp", axis=0, tiled=True),
        lax.all_gather(w_beta, "fsdp", axis=0, tiled=True),
        lax.all_gather(w_decay, "fsdp", axis=0, tiled=True),
        lax.all_gather(conv_query, "fsdp", axis=1, tiled=True),
        lax.all_gather(conv_key, "fsdp", axis=1, tiled=True),
        lax.all_gather(conv_value, "fsdp", axis=1, tiled=True),
        lax.all_gather(gain_mix, "fsdp", axis=0, tiled=True),
        lax.all_gather(gain_head, "fsdp", axis=0, tiled=True),
        lax.all_gather(w_out, "fsdp", axis=1, tiled=True),
    )
    group_tokens, mix_gain, head_gain = (
        lax.all_gather(tokens, "tp", axis=0, tiled=True),
        lax.all_gather(mix_gain_part, "tp", axis=0, tiled=True),
        lax.all_gather(head_gain_part, "tp", axis=0, tiled=True),
    )
    shard_rows = tokens.shape[0]
    key_width = query_full.shape[1]
    value_width = value_full.shape[1]
    head_count = beta_full.shape[1]
    edges = [
        key_width,
        2 * key_width,
        2 * key_width + value_width,
        2 * key_width + 2 * value_width,
        2 * key_width + 2 * value_width + head_count,
    ]
    combined = jnp.concatenate(
        [query_full, key_full, value_full, outgate_full, beta_full, decay_full], axis=1
    )
    group_float = group_tokens.astype(jnp.float32)
    mix_scale = norm_scale(group_float)
    mix_gain_f = mix_gain.astype(jnp.float32)
    normed = (group_float * mix_scale * mix_gain_f).astype(jnp.bfloat16)
    projected = jnp.dot(normed, combined, preferred_element_type=jnp.float32)
    query_proj, key_proj, value_proj, gate_proj, beta_logit, decay_logit = jnp.split(
        projected, edges, axis=1
    )
    prepared, pull_prepare = jax.vjp(
        prepare,
        query_proj,
        key_proj,
        value_proj,
        beta_logit,
        decay_logit,
        convq_full.astype(jnp.float32),
        convk_full.astype(jnp.float32),
        convv_full.astype(jnp.float32),
        decay_log.astype(jnp.float32),
        decay_bias.astype(jnp.float32),
    )
    query_rows, key_rows, value_rows, beta_rows, decay_rows = prepared
    mixed, pull_delta = jax.vjp(
        run_delta,
        round_trip(query_rows),
        round_trip(key_rows),
        round_trip(value_rows),
        beta_rows,
        decay_rows,
    )
    head_gain_f = head_gain.astype(jnp.float32)
    gated_float, pull_finish = jax.vjp(finish, mixed, gate_proj, head_gain_f)
    gated = gated_float.astype(jnp.bfloat16)
    hidden_state = tokens.astype(jnp.float32) + lax.psum_scatter(
        jnp.dot(gated, out_full, preferred_element_type=jnp.float32).astype(jnp.bfloat16),
        "tp",
        scatter_dimension=0,
        tiled=True,
    ).astype(jnp.float32)
    gate_full, up_full, down_full, ff_gain_part = (
        lax.all_gather(w_gate, "fsdp", axis=0, tiled=True),
        lax.all_gather(w_up, "fsdp", axis=0, tiled=True),
        lax.all_gather(w_down, "fsdp", axis=1, tiled=True),
        lax.all_gather(gain_ff, "fsdp", axis=0, tiled=True),
    )
    sent = hidden_state.astype(jnp.bfloat16)
    group_hidden, ff_gain = (
        lax.all_gather(sent, "tp", axis=0, tiled=True),
        lax.all_gather(ff_gain_part, "tp", axis=0, tiled=True),
    )
    hidden_float = group_hidden.astype(jnp.float32)
    ff_scale = norm_scale(hidden_float)
    ff_gain_f = ff_gain.astype(jnp.float32)
    ff_normed = (hidden_float * ff_scale * ff_gain_f).astype(jnp.bfloat16)
    ff_weights = jnp.concatenate([gate_full, up_full], axis=1)
    ff_width = gate_full.shape[1]
    activations = jnp.dot(ff_normed, ff_weights, preferred_element_type=jnp.float32)
    gate_act = activations[:, :ff_width]
    up_act = activations[:, ff_width:]
    inner = (jax.nn.silu(gate_act) * up_act).astype(jnp.bfloat16)
    ff_branch = lax.psum_scatter(
        jnp.dot(inner, down_full, preferred_element_type=jnp.float32).astype(jnp.bfloat16),
        "tp",
        scatter_dimension=0,
        tiled=True,
    ).astype(jnp.float32)
    row_start = lax.axis_index("tp") * shard_rows
    live = row_start + jnp.arange(shard_rows, dtype=jnp.int32) < lengths[0]
    layer_out = jnp.where(live[:, None], hidden_state + ff_branch, 0.0).astype(jnp.bfloat16)
    grad_out = jnp.where(live[:, None], cotangent.astype(jnp.float32), 0.0)
    group_grad_ff = lax.all_gather(grad_out.astype(jnp.bfloat16), "tp", axis=0, tiled=True)
    grad_inner = lax.dot_general(
        group_grad_ff, down_full, contract_cols, preferred_element_type=jnp.float32
    )
    down_grad = lax.dot_general(
        inner, group_grad_ff, contract_rows, preferred_element_type=jnp.float32
    )
    gate_sigmoid = jax.nn.sigmoid(gate_act)
    grad_gate = grad_inner * up_act * gate_sigmoid * (1.0 + gate_act * (1.0 - gate_sigmoid))
    grad_up = grad_inner * gate_act * gate_sigmoid
    grad_acts = jnp.concatenate([grad_gate, grad_up], axis=1).astype(jnp.bfloat16)
    ff_weight_grad = lax.dot_general(
        ff_normed, grad_acts, contract_rows, preferred_element_type=jnp.float32
    )
    grad_ff_normed = lax.dot_general(
        grad_acts, ff_weights, contract_cols, preferred_element_type=jnp.float32
    )
    sent_grad_part, ff_gain_grad_part = norm_back(grad_ff_normed, hidden_float, ff_scale, ff_gain_f)
    grad_sent, ff_gain_grad_tp = (
        lax.psum_scatter(
            sent_grad_part.astype(jnp.bfloat16), "tp", scatter_dimension=0, tiled=True
        ).astype(jnp.float32),
        lax.psum_scatter(
            ff_gain_grad_part.astype(jnp.bfloat16), "tp", scatter_dimension=0, tiled=True
        ).astype(jnp.float32),
    )
    gate_grad = ff_weight_grad[:, :ff_width]
    up_grad = ff_weight_grad[:, ff_width:]
    grad_hidden = grad_out + grad_sent
    group_grad_branch = lax.all_gather(grad_hidden.astype(jnp.bfloat16), "tp", axis=0, tiled=True)
    out_grad = lax.dot_general(
        gated, group_grad_branch, contract_rows, preferred_element_type=jnp.float32
    )
    grad_gated = lax.dot_general(
        group_grad_branch, out_full, contract_cols, preferred_element_type=jnp.float32
    )
    grad_mixed, grad_gate_proj, head_gain_grad_part = pull_finish(grad_gated)
    delta_grads = pull_delta(grad_mixed)
    (
        grad_query_proj,
        grad_key_proj,
        grad_value_proj,
        grad_beta_logit,
        grad_decay_logit,
        convq_grad,
        convk_grad,
        convv_grad,
        decay_log_grad,
        decay_bias_grad,
    ) = pull_prepare(delta_grads)
    grad_projected = jnp.concatenate(
        [
            grad_query_proj,
            grad_key_proj,
            grad_value_proj,
            grad_gate_proj,
            grad_beta_logit,
            grad_decay_logit,
        ],
        axis=1,
    ).astype(jnp.bfloat16)
    combined_grad = lax.dot_general(
        normed, grad_projected, contract_rows, preferred_element_type=jnp.float32
    )
    grad_normed = lax.dot_general(
        grad_projected, combined, contract_cols, preferred_element_type=jnp.float32
    )
    tokens_grad_part, mix_gain_grad_part = norm_back(
        grad_normed, group_float, mix_scale, mix_gain_f
    )
    grad_tokens, mix_gain_grad_tp, head_gain_grad_tp = (
        lax.psum_scatter(
            tokens_grad_part.astype(jnp.bfloat16), "tp", scatter_dimension=0, tiled=True
        ).astype(jnp.float32),
        lax.psum_scatter(
            mix_gain_grad_part.astype(jnp.bfloat16), "tp", scatter_dimension=0, tiled=True
        ).astype(jnp.float32),
        lax.psum_scatter(
            head_gain_grad_part.astype(jnp.bfloat16), "tp", scatter_dimension=0, tiled=True
        ).astype(jnp.float32),
    )
    input_grad = grad_hidden + grad_tokens
    query_grad, key_grad, value_grad, outgate_grad, beta_grad, decay_grad = jnp.split(
        combined_grad, edges, axis=1
    )
    all_sums = (
        lax.psum_scatter(query_grad, "fsdp", scatter_dimension=0, tiled=True),
        lax.psum_scatter(key_grad, "fsdp", scatter_dimension=0, tiled=True),
        lax.psum_scatter(value_grad, "fsdp", scatter_dimension=0, tiled=True),
        lax.psum_scatter(outgate_grad, "fsdp", scatter_dimension=0, tiled=True),
        lax.psum_scatter(beta_grad, "fsdp", scatter_dimension=0, tiled=True),
        lax.psum_scatter(decay_grad, "fsdp", scatter_dimension=0, tiled=True),
        lax.psum_scatter(convq_grad, "fsdp", scatter_dimension=1, tiled=True),
        lax.psum_scatter(convk_grad, "fsdp", scatter_dimension=1, tiled=True),
        lax.psum_scatter(convv_grad, "fsdp", scatter_dimension=1, tiled=True),
        lax.psum_scatter(mix_gain_grad_tp, "fsdp", scatter_dimension=0, tiled=True),
        lax.psum_scatter(head_gain_grad_tp, "fsdp", scatter_dimension=0, tiled=True),
        lax.psum_scatter(out_grad, "fsdp", scatter_dimension=1, tiled=True),
        lax.psum_scatter(gate_grad, "fsdp", scatter_dimension=0, tiled=True),
        lax.psum_scatter(up_grad, "fsdp", scatter_dimension=0, tiled=True),
        lax.psum_scatter(down_grad, "fsdp", scatter_dimension=1, tiled=True),
        lax.psum_scatter(ff_gain_grad_tp, "fsdp", scatter_dimension=0, tiled=True),
    )
    mix_sums = all_sums[:12]
    ff_sums = all_sums[12:]
    decay_sums = lax.psum((decay_log_grad, decay_bias_grad), "fsdp")
    return (
        layer_out,
        input_grad,
        mix_sums[9],
        mix_sums[0],
        mix_sums[1],
        mix_sums[2],
        mix_sums[3],
        mix_sums[4],
        mix_sums[5],
        mix_sums[6],
        mix_sums[7],
        mix_sums[8],
        decay_sums[0],
        decay_sums[1],
        mix_sums[10],
        mix_sums[11],
        ff_sums[3],
        ff_sums[0],
        ff_sums[1],
        ff_sums[2],
    )


def solution(mesh):
    placed = (
        P(("fsdp", "tp"), None),
        P("fsdp"),
        P(("tp", "fsdp")),
        P("fsdp", "tp"),
        P("fsdp", "tp"),
        P("fsdp", "tp"),
        P("fsdp", "tp"),
        P("fsdp", "tp"),
        P("fsdp", "tp"),
        P(None, ("tp", "fsdp")),
        P(None, ("tp", "fsdp")),
        P(None, ("tp", "fsdp")),
        P("tp"),
        P("tp"),
        P(("tp", "fsdp")),
        P("tp", "fsdp"),
        P(("tp", "fsdp")),
        P("fsdp", "tp"),
        P("fsdp", "tp"),
        P("tp", "fsdp"),
        P(("fsdp", "tp"), None),
    )
    return jax.shard_map(
        body,
        mesh=mesh,
        in_specs=placed,
        out_specs=(
            P(("fsdp", "tp"), None),
            P(("fsdp", "tp"), None),
            P(("tp", "fsdp")),
            P("fsdp", "tp"),
            P("fsdp", "tp"),
            P("fsdp", "tp"),
            P("fsdp", "tp"),
            P("fsdp", "tp"),
            P("fsdp", "tp"),
            P(None, ("tp", "fsdp")),
            P(None, ("tp", "fsdp")),
            P(None, ("tp", "fsdp")),
            P("tp"),
            P("tp"),
            P(("tp", "fsdp")),
            P("tp", "fsdp"),
            P(("tp", "fsdp")),
            P("fsdp", "tp"),
            P("fsdp", "tp"),
            P("tp", "fsdp"),
        ),
        check_vma=False,
    )
```

profile of v0, /device:TPU:12, one launch (start us, length us, event | category | flops | bytes accessed | tf_op | source)
XLA Modules:
  0.0 1745.7 jit_solution(12308930941679170728)
XLA Ops:
  15.4 13.2 all-reduce.36
  28.6 8.2 all-gather
  36.8 10.5 all_gather.72
  47.4 10.7 all_gather.73
  58.0 8.4 all_gather.76
  66.7 8.2 all_gather.77
  75.0 8.6 all-gather.1
  84.4 8.3 all-gather.2
  92.8 8.6 all-gather.3
  103.0 10.8 all-reduce.27
  113.8 6.3 concatenate.23
  122.4 5.8 fusion.137
  134.1 6.8 fusion.230
  167.4 7.2 multiply_convert_fusion.4
  193.7 3.7 convolution_add_fusion.9
  200.6 3.8 fusion.75
  207.5 127.8 %while.44 = (s32[]{:T(128)}, f32[2,256,128]{2,1,0:T(8,128)S(1)}, f32[16,64,2,256]{3,1,2,0:T(8,128)}, f32[16,2,256,128]{3,2,1,0:T(8,128)}, f32[16,2]{1,0:T(8,128)...) while((s32[]{:T(128)}, f32[2,256,128]{2,1,0:T(8,128)S(1)}, ...), condition=%wide.region_5.6_spmd.clone, body=%wide.region_4.5_spmd.clone.sunk | while | flops 176652288 | bytes 2757802 | solution.py:132
  335.3 4.9 copy.502
  340.1 5.2 reshape.436
  347.4 4.5 fusion.220
  351.9 4.2 convolution_convert_fusion
  357.5 40.5 %reduce-scatter.28.cloned.1.call-done = bf16[256,1024]{1,0:T(8,128)(2,1)} async-done(((bf16[1024,1024]{1,0:T(8,128)(2,1)}), bf16[256,1024]{1,0:T(8,128)(2,1)}) %reduce-scatter.28.cloned.1.call-update) | async-done | bytes 524304 | tf_op jit(solution)/shard_map/reduce_scatter | solution.py:267
  403.8 8.9 all-gather.4
  412.7 12.1 all-gather.26.cloned.1.call-done
  427.4 24.5 %all-gather.28.cloned.1.call-done = bf16[1024,704]{0,1:T(8,128)(2,1)} async-done(((bf16[128,704]{0,1:T(8,128)(2,1)}), bf16[1024,704]{0,1:T(8,128)(2,1)}) %all-gather.28.cloned.1.call-update) | async-done | bytes 1441808 | tf_op jit(solution)/shard_map/all_gather | solution.py:275
  454.5 43.6 %all-gather.24.cloned.1.call-done = bf16[1024,1024]{1,0:T(8,128)(2,1)} async-done(((bf16[256,1024]{1,0:T(8,128)(2,1)}), bf16[1024,1024]{1,0:T(8,128)(2,1)}) %all-gather.24.cloned.1.call-update) | async-done | bytes 2097168 | tf_op jit(solution)/shard_map/all_gather | solution.py:281
  500.3 7.4 fusion.133
  507.7 17.4 all-gather.30.cloned.1.call-done
  525.1 46.0 %all-gather.32.cloned.1.call-done = bf16[1024,1024]{1,0:T(8,128)(2,1)} async-done(((bf16[256,1024]{1,0:T(8,128)(2,1)}), bf16[1024,1024]{1,0:T(8,128)(2,1)}) %all-gather.32.cloned.1.call-update) | async-done | bytes 2097168 | tf_op jit(solution)/shard_map/all_gather | solution.py:304
  571.1 7.7 multiply_convert_fusion.1
  578.8 4.3 fusion.62
  585.5 43.0 %reduce-scatter.32.cloned.1.call-done = bf16[256,1024]{1,0:T(8,128)(2,1)} async-done(((bf16[1024,1024]{1,0:T(8,128)(2,1)}), bf16[256,1024]{1,0:T(8,128)(2,1)}) %reduce-scatter.32.cloned.1.call-update) | async-done | bytes 524304 | tf_op jit(solution)/shard_map/reduce_scatter | solution.py:323
  631.0 6.2 fusion.76
  637.2 3.8 fusion.222
  648.8 26.5 %all-gather.34.cloned.1.call-done = bf16[1024,1024]{1,0:T(8,128)(2,1)} async-done(((bf16[256,1024]{1,0:T(8,128)(2,1)}), bf16[1024,1024]{1,0:T(8,128)(2,1)}) %all-gather.34.cloned.1.call-update) | async-done | bytes 2097168 | tf_op jit(solution)/shard_map/all_gather | solution.py:333
  675.3 4.5 fusion.235
  686.2 8.6 multiply_reduce_fusion.2
  697.2 6.4 add_add_fusion
  710.8 378.5 %while.45 = (s32[]{:T(128)}, f32[2,256,128]{2,1,0:T(8,128)}, f32[16,2,64,128]{3,2,1,0:T(8,128)}, f32[16,2,64,256]{3,2,1,0:T(8,128)}, f32[16,2,64,64]{2,3,1,0:T(8...) while((s32[]{:T(128)}, f32[2,256,128]{2,1,0:T(8,128)}, ...), condition=%wide.region_16.17_spmd.clone, body=%wide.region_13.16_spmd.clone.sunk | while | flops 403308416 | bytes 8363019 | solution.py:132
  1092.7 3.7 fusion.78
  1149.1 4.9 copy.519
  1153.9 5.0 reshape.455
  1173.2 4.9 multiply_reduce_fusion.12
  1186.1 8.4 multiply_reduce_fusion.6
  1215.6 5.8 fusion.71
  1225.5 15.0 concatenate.29
  1240.5 5.7 fusion.135
  1254.9 4.8 fusion.218
  1260.5 5.0 convolution_convert_fusion.1
  1265.8 7.8 fusion.55
  1277.6 4.6 fusion.242
  1283.5 4.2 fusion.241
  1294.3 10.1 all-reduce.37
  1304.6 12.3 all-reduce.35
  1322.9 27.1 %reduce-scatter.52.cloned.1.call-done = f32[128,2]{1,0:T(8,128)} async-done(((f32[1024,2]{1,0:T(8,128)}), f32[128,2]{1,0:T(8,128)}) %reduce-scatter.52.cloned.1.call-update) | async-done | bytes 1040
  1351.4 35.8 %reduce-scatter.54.cloned.1.call-done = f32[128,2]{1,0:T(8,128)} async-done(((f32[1024,2]{1,0:T(8,128)}), f32[128,2]{1,0:T(8,128)}) %reduce-scatter.54.cloned.1.call-update) | async-done | bytes 1040
  1388.6 37.6 %reduce-scatter.36.cloned.1.call-done = f32[128,256]{0,1:T(8,128)} async-done(((f32[1024,256]{0,1:T(8,128)}), f32[128,256]{0,1:T(8,128)}) %reduce-scatter.36.cloned.1.call-update) | async-done | bytes 131088 | tf_op jit(solution)/shard_map/reduce_scatter | solution.py:390
  1427.9 38.1 %reduce-scatter.38.cloned.1.call-done = f32[128,256]{0,1:T(8,128)} async-done(((f32[1024,256]{0,1:T(8,128)}), f32[128,256]{0,1:T(8,128)}) %reduce-scatter.38.cloned.1.call-update) | async-done | bytes 131088 | tf_op jit(solution)/shard_map/reduce_scatter | solution.py:391
  1467.6 42.8 %reduce-scatter.40.cloned.1.call-done = f32[128,512]{0,1:T(8,128)} async-done(((f32[1024,512]{0,1:T(8,128)}), f32[128,512]{0,1:T(8,128)}) %reduce-scatter.40.cloned.1.call-update) | async-done | bytes 262160 | tf_op jit(solution)/shard_map/reduce_scatter | solution.py:392
  1512.2 42.6 %reduce-scatter.42.cloned.1.call-done = f32[128,512]{0,1:T(8,128)} async-done(((f32[1024,512]{0,1:T(8,128)}), f32[128,512]{0,1:T(8,128)}) %reduce-scatter.42.cloned.1.call-update) | async-done | bytes 262160 | tf_op jit(solution)/shard_map/reduce_scatter | solution.py:393
  1556.6 43.2 %reduce-scatter.30.cloned.1.call-done = bf16[256,1024]{1,0:T(8,128)(2,1)} async-done(((bf16[1024,1024]{1,0:T(8,128)(2,1)}), bf16[256,1024]{1,0:T(8,128)(2,1)}) %reduce-scatter.30.cloned.1.call-update) | async-done | bytes 524304 | tf_op jit(solution)/shard_map/reduce_scatter | solution.py:294
  1599.8 45.1 %reduce-scatter.34.cloned.1.call-done = bf16[256,1024]{1,0:T(8,128)(2,1)} async-done(((bf16[1024,1024]{1,0:T(8,128)(2,1)}), bf16[256,1024]{1,0:T(8,128)(2,1)}) %reduce-scatter.34.cloned.1.call-update) | async-done | bytes 524304 | tf_op jit(solution)/shard_map/reduce_scatter | solution.py:375
  1648.1 45.4 %reduce-scatter.50.cloned.1.call-done = f32[704,128]{1,0:T(8,128)} async-done(((f32[704,1024]{1,0:T(8,128)}), f32[704,128]{1,0:T(8,128)}) %reduce-scatter.50.cloned.1.call-update) | async-done | bytes 360464 | tf_op jit(solution)/shard_map/reduce_scatter | solution.py:404
  1693.5 44.9 %reduce-scatter.44.cloned.1.call-done = f32[512,128]{1,0:T(8,128)} async-done(((f32[512,1024]{1,0:T(8,128)}), f32[512,128]{1,0:T(8,128)}) %reduce-scatter.44.cloned.1.call-update) | async-done | bytes 262160 | tf_op jit(solution)/shard_map/reduce_scatter | solution.py:401
  (1203 shorter events, 757.8 us)
Async XLA Ops:
  7.2 50.9 %copy-start.147 = (bf16[128,2]{0,1:T(2,128)(2,1)S(1)}, bf16[128,2]{0,1:T(2,128)(2,1)}, u32[]{:S(2)}) copy-start(bf16[128,2]{0,1:T(2,128)(2,1)} %param.32) | copy-start | bytes 1540
  7.2 59.5 %copy-start.148 = (bf16[128,2]{0,1:T(2,128)(2,1)S(1)}, bf16[128,2]{0,1:T(2,128)(2,1)}, u32[]{:S(2)}) copy-start(bf16[128,2]{0,1:T(2,128)(2,1)} %param.33) | copy-start | bytes 1540
  7.2 67.8 %copy-start.144 = (bf16[4,32]{1,0:T(4,128)(2,1)S(1)}, bf16[4,32]{1,0:T(4,128)(2,1)}, u32[]{:S(2)}) copy-start(bf16[4,32]{1,0:T(4,128)(2,1)} %param.35) | copy-start | bytes 772
  7.2 77.1 %copy-start.149 = (bf16[2]{0:T(256)(128)(2,1)S(1)}, bf16[2]{0:T(256)(128)(2,1)}, u32[]{:S(2)}) copy-start(bf16[2]{0:T(256)(128)(2,1)} %param.38) | copy-start | bytes 16
  7.2 77.1 %copy-start.150 = (bf16[2]{0:T(256)(128)(2,1)S(1)}, bf16[2]{0:T(256)(128)(2,1)}, u32[]{:S(2)}) copy-start(bf16[2]{0:T(256)(128)(2,1)} %param.37) | copy-start | bytes 16
  7.2 77.1 %copy-start.145 = (bf16[4,64]{1,0:T(4,128)(2,1)S(1)}, bf16[4,64]{1,0:T(4,128)(2,1)}, u32[]{:S(2)}) copy-start(bf16[4,64]{1,0:T(4,128)(2,1)} %param.36) | copy-start | bytes 1540
  7.3 85.5 %copy-start.146 = (bf16[4,32]{1,0:T(4,128)(2,1)S(1)}, bf16[4,32]{1,0:T(4,128)(2,1)}, u32[]{:S(2)}) copy-start(bf16[4,32]{1,0:T(4,128)(2,1)} %param.34) | copy-start | bytes 772
  7.3 106.5 %all-gather.18.cloned.1.call-start = ((), (), s32[]{:S(2)}) async-start(), calls=%async_computation.18 | async-start | bytes 1179648 | tf_op jit(solution)/shard_map/all_gather | solution.py:204
  8.0 105.8 %all-gather.20.cloned.1.call-start = ((), (), s32[]{:S(2)}) async-start(), calls=%async_computation.19 | async-start | bytes 1179648 | tf_op jit(solution)/shard_map/all_gather | solution.py:205
  8.7 111.4 %all-gather.16.cloned.1.call-start = ((), (), s32[]{:S(2)}) async-start(), calls=%async_computation.17 | async-start | bytes 2621440 | tf_op jit(solution)/shard_map/all_gather | solution.py:216
  9.5 342.4 %all-gather.22.cloned.1.call-start = ((), (), s32[]{:S(2)}) async-start(), calls=%async_computation.20 | async-start | bytes 1179648 | tf_op jit(solution)/shard_map/all_gather | solution.py:213
  10.1 387.9 %reduce-scatter.28.cloned.1.call-start = ((), (), s32[]{:S(2)}) async-start(), calls=%async_computation.21 | async-start | bytes 2621440 | tf_op jit(solution)/shard_map/reduce_scatter | solution.py:267
  10.1 141.3 %copy-start.80 = (pred[64,64]{0,1:T(8,128)(4,1)}, pred[64,64]{0,1:T(8,128)(4,1)S(1)}, u32[]{:S(2)}) copy-start(pred[64,64]{0,1:T(8,128)(4,1)S(1)} %get-tuple-element.935) | copy-start | bytes 12292
  10.2 141.3 %copy-start.82 = (f32[64,64]{0,1:T(8,128)}, f32[64,64]{0,1:T(8,128)S(1)}, u32[]{:S(2)}) copy-start(f32[64,64]{0,1:T(8,128)S(1)} %get-tuple-element.936) | copy-start | bytes 49156
  10.2 195.5 %copy-start.91 = (pred[64,64]{0,1:T(8,128)(4,1)}, pred[64,64]{0,1:T(8,128)(4,1)S(1)}, u32[]{:S(2)}) copy-start(pred[64,64]{0,1:T(8,128)(4,1)S(1)} %iota_compare_fusion) | copy-start | bytes 12292
  36.8 85.6 %copy-start.116 = (f32[4,1,256]{2,1,0:T(1,128)}, f32[4,1,256]{2,1,0:T(1,128)S(1)}, u32[]{:S(2)}) copy-start(f32[4,1,256]{2,1,0:T(1,128)S(1)} %convert_element_type.165) | copy-start | bytes 12292
  84.3 56.8 %copy-start.121 = (f32[1,256]{1,0:T(1,128)}, f32[1,256]{1,0:T(1,128)S(1)}, u32[]{:S(2)}) copy-start(f32[1,256]{1,0:T(1,128)S(1)} %get-tuple-element.914) | copy-start | bytes 3076
  84.3 47.1 %copy-start.138 = (f32[2]{0:T(128)}, f32[2]{0:T(128)S(1)}, u32[]{:S(2)}) copy-start(f32[2]{0:T(128)S(1)} %convert_element_type.131) | copy-start | bytes 28
  84.3 47.1 %copy-start.140 = (f32[2]{0:T(128)}, f32[2]{0:T(128)S(1)}, u32[]{:S(2)}) copy-start(f32[2]{0:T(128)S(1)} %fusion.194) | copy-start | bytes 28
  92.8 74.6 %copy-start.106 = (f32[1,512]{1,0:T(1,128)}, f32[1,512]{1,0:T(1,128)S(1)}, u32[]{:S(2)}) copy-start(f32[1,512]{1,0:T(1,128)S(1)} %get-tuple-element.906) | copy-start | bytes 6148
  92.8 74.6 %copy-start.108 = (f32[1,512]{1,0:T(1,128)}, f32[1,512]{1,0:T(1,128)S(1)}, u32[]{:S(2)}) copy-start(f32[1,512]{1,0:T(1,128)S(1)} %get-tuple-element.907) | copy-start | bytes 6148
  92.8 74.6 %copy-start.110 = (f32[1,512]{1,0:T(1,128)}, f32[1,512]{1,0:T(1,128)S(1)}, u32[]{:S(2)}) copy-start(f32[1,512]{1,0:T(1,128)S(1)} %get-tuple-element.908) | copy-start | bytes 6148
  92.8 74.6 %copy-start.112 = (f32[1,512]{1,0:T(1,128)}, f32[1,512]{1,0:T(1,128)S(1)}, u32[]{:S(2)}) copy-start(f32[1,512]{1,0:T(1,128)S(1)} %get-tuple-element.909) | copy-start | bytes 6148
  113.7 233.7 %copy-start.114 = (f32[1,2,2,128]{3,1,2,0:T(2,128)}, f32[1,2,2,128]{3,1,2,0:T(2,128)S(1)}, u32[]{:S(2)}) copy-start(f32[1,2,2,128]{3,1,2,0:T(2,128)S(1)} %copy.588) | copy-start | bytes 6148
  129.4 11.7 copy-start.43
  133.6 66.9 %copy-start.86 = (f32[16,64,2]{1,2,0:T(2,128)}, f32[16,64,2]{1,2,0:T(2,128)S(1)}, u32[]{:S(2)}) copy-start(f32[16,64,2]{1,2,0:T(2,128)S(1)} %copy.372) | copy-start | bytes 24580
  167.4 30.0 %copy-start.84 = (f32[16,64,2]{1,2,0:T(2,128)}, f32[16,64,2]{1,2,0:T(2,128)S(1)}, u32[]{:S(2)}) copy-start(f32[16,64,2]{1,2,0:T(2,128)S(1)} %copy.377) | copy-start | bytes 24580
  189.1 15.3 copy-start.89
  356.1 47.7 %copy-start.152 = (bf16[256]{0:T(256)(128)(2,1)S(1)}, bf16[256]{0:T(256)(128)(2,1)}, u32[]{:S(2)}) copy-start(bf16[256]{0:T(256)(128)(2,1)} %get-tuple-element.845) | copy-start | bytes 1540
  356.1 68.7 %all-gather.26.cloned.1.call-start = ((), (), s32[]{:S(2)}) async-start(), calls=%async_computation.23 | async-start | bytes 1622016 | tf_op jit(solution)/shard_map/all_gather | solution.py:274
  356.7 95.2 %all-gather.28.cloned.1.call-start = ((), (), s32[]{:S(2)}) async-start(), calls=%async_computation.24 | async-start | bytes 1622016 | tf_op jit(solution)/shard_map/all_gather | solution.py:275
  357.4 140.6 %all-gather.24.cloned.1.call-start = ((), (), s32[]{:S(2)}) async-start(), calls=%async_computation.22 | async-start | bytes 2621440 | tf_op jit(solution)/shard_map/all_gather | solution.py:281
  400.2 124.9 %all-gather.30.cloned.1.call-start = ((), (), s32[]{:S(2)}) async-start(), calls=%async_computation.25 | async-start | bytes 1622016 | tf_op jit(solution)/shard_map/all_gather | solution.py:276
  400.9 170.1 %all-gather.32.cloned.1.call-start = ((), (), s32[]{:S(2)}) async-start(), calls=%async_computation.27 | async-start | bytes 2621440 | tf_op jit(solution)/shard_map/all_gather | solution.py:304
  401.7 226.8 %copy-start.136 = (pred[256]{0:T(512)(128)(4,1)}, pred[256]{0:T(512)(128)(4,1)S(1)}, u32[]{:S(2)}) copy-start(pred[256]{0:T(512)(128)(4,1)S(1)} %add_compare_fusion) | copy-start | bytes 772
  403.7 224.8 %reduce-scatter.32.cloned.1.call-start = ((), (), s32[]{:S(2)}) async-start(), calls=%async_computation.28 | async-start | bytes 2621440 | tf_op jit(solution)/shard_map/reduce_scatter | solution.py:323
  585.4 89.8 %all-gather.34.cloned.1.call-start = ((), (), s32[]{:S(2)}) async-start(), calls=%async_computation.29 | async-start | bytes 2621440 | tf_op jit(solution)/shard_map/all_gather | solution.py:333
  630.7 659.8 %reduce-scatter.46.cloned.1.call-start = ((), (), s32[]{:S(2)}) async-start(), calls=%async_computation.36 | async-start | bytes 3538944 | tf_op jit(solution)/shard_map/reduce_scatter | solution.py:402
  641.0 651.4 %reduce-scatter.48.cloned.1.call-start = ((), (), s32[]{:S(2)}) async-start(), calls=%async_computation.37 | async-start | bytes 3538944 | tf_op jit(solution)/shard_map/reduce_scatter | solution.py:403
  648.5 670.2 %reduce-scatter.58.cloned.1.call-start = ((), (), s32[]{:S(2)}) async-start(), calls=%async_computation.42 | async-start | bytes 147456
  767.7 9.2 copy-start.56
  933.3 9.2 copy-start.56
  1186.1 10.7 copy-start.51
  1204.3 115.8 %reduce-scatter.56.cloned.1.call-start = ((), (), s32[]{:S(2)}) async-start(), calls=%async_computation.41 | async-start | bytes 147456
  1208.4 113.1 %reduce-scatter.60.cloned.1.call-start = ((), (), s32[]{:S(2)}) async-start(), calls=%async_computation.43 | async-start | bytes 294912
  1214.2 135.7 %reduce-scatter.52.cloned.1.call-start = ((), (), s32[]{:S(2)}) async-start(), calls=%async_computation.39 | async-start | bytes 589824
  1225.5 15.1 copy-start.53
  1225.5 15.1 copy-start.117
  1225.5 15.1 copy-start.119
  1249.9 137.3 %reduce-scatter.54.cloned.1.call-start = ((), (), s32[]{:S(2)}) async-start(), calls=%async_computation.40 | async-start | bytes 589824
  1251.0 175.2 %reduce-scatter.36.cloned.1.call-start = ((), (), s32[]{:S(2)}) async-start(), calls=%async_computation.31 | async-start | bytes 1179648 | tf_op jit(solution)/shard_map/reduce_scatter | solution.py:390
  1254.2 211.8 %reduce-scatter.38.cloned.1.call-start = ((), (), s32[]{:S(2)}) async-start(), calls=%async_computation.32 | async-start | bytes 1179648 | tf_op jit(solution)/shard_map/reduce_scatter | solution.py:391
  1254.9 255.5 %reduce-scatter.40.cloned.1.call-start = ((), (), s32[]{:S(2)}) async-start(), calls=%async_computation.33 | async-start | bytes 2359296 | tf_op jit(solution)/shard_map/reduce_scatter | solution.py:392
  1259.7 295.1 %reduce-scatter.42.cloned.1.call-start = ((), (), s32[]{:S(2)}) async-start(), calls=%async_computation.34 | async-start | bytes 2359296 | tf_op jit(solution)/shard_map/reduce_scatter | solution.py:393
  1260.5 339.4 %reduce-scatter.30.cloned.1.call-start = ((), (), s32[]{:S(2)}) async-start(), calls=%async_computation.26 | async-start | bytes 2621440 | tf_op jit(solution)/shard_map/reduce_scatter | solution.py:294
  1265.5 379.4 %reduce-scatter.34.cloned.1.call-start = ((), (), s32[]{:S(2)}) async-start(), calls=%async_computation.30 | async-start | bytes 2621440 | tf_op jit(solution)/shard_map/reduce_scatter | solution.py:375
  1276.0 417.5 %reduce-scatter.50.cloned.1.call-start = ((), (), s32[]{:S(2)}) async-start(), calls=%async_computation.38 | async-start | bytes 3244032 | tf_op jit(solution)/shard_map/reduce_scatter | solution.py:404
  1282.3 456.1 %reduce-scatter.44.cloned.1.call-start = ((), (), s32[]{:S(2)}) async-start(), calls=%async_computation.35 | async-start | bytes 2359296 | tf_op jit(solution)/shard_map/reduce_scatter | solution.py:401
  1287.6 17.0 copy-start.151
  1287.7 357.3 %copy-start.59 = (bf16[256,1024]{1,0:T(8,128)(2,1)S(1)}, bf16[256,1024]{1,0:T(8,128)(2,1)}, u32[]{:S(2)}) copy-start(bf16[256,1024]{1,0:T(8,128)(2,1)} %param.25) | copy-start | bytes 1572868
  1287.7 357.3 %copy-start.60 = (bf16[256,1024]{1,0:T(8,128)(2,1)S(1)}, bf16[256,1024]{1,0:T(8,128)(2,1)}, u32[]{:S(2)}) copy-start(bf16[256,1024]{1,0:T(8,128)(2,1)} %param.45) | copy-start | bytes 1572868
  1287.7 357.3 %copy-start.72 = (bf16[256,1024]{1,0:T(8,128)(2,1)S(1)}, bf16[256,1024]{1,0:T(8,128)(2,1)}, u32[]{:S(2)}) copy-start(bf16[256,1024]{1,0:T(8,128)(2,1)} %reduce-scatter.28.cloned.1.call-done) | copy-start | bytes 1572868
  1287.7 357.3 %copy-start.73 = (bf16[256,1024]{1,0:T(8,128)(2,1)S(1)}, bf16[256,1024]{1,0:T(8,128)(2,1)}, u32[]{:S(2)}) copy-start(bf16[256,1024]{1,0:T(8,128)(2,1)} %reduce-scatter.32.cloned.1.call-done) | copy-start | bytes 1572868
  1287.7 357.3 %copy-start.137 = (pred[256]{0:T(512)(128)(4,1)S(1)}, pred[256]{0:T(512)(128)(4,1)}, u32[]{:S(2)}) copy-start(pred[256]{0:T(512)(128)(4,1)} %copy-done.136) | copy-start | bytes 772
  (193 other events, 1048.1 us)
Sparse Core Ops, SparseCore 0:
  10.0 24.4 all-gather.17
  36.4 23.7 all-gather.19
  61.7 43.9 all-gather.15
  107.5 23.4 all-gather.21
  356.2 41.7 reduce-scatter.27
  399.7 25.0 all-gather.25
  426.7 25.1 all-gather.27
  453.5 44.5 all-gather.23
  499.9 25.0 all-gather.29
  526.5 44.5 all-gather.31
  585.5 42.8 reduce-scatter.31
  630.8 44.3 all-gather.33
  678.6 46.1 reduce-scatter.45
  728.1 46.1 reduce-scatter.47
  1204.4 33.6 reduce-scatter.57
  1241.5 33.5 reduce-scatter.55
  1278.6 33.6 reduce-scatter.59
  1315.8 34.0 reduce-scatter.51
  1353.0 34.1 reduce-scatter.53
  1390.2 35.9 reduce-scatter.35
  1430.0 35.9 reduce-scatter.37
  1469.3 41.0 reduce-scatter.39
  1513.7 41.0 reduce-scatter.41
  1557.0 42.8 reduce-scatter.29
  1602.1 42.8 reduce-scatter.33
  1648.8 44.6 reduce-scatter.49
  1697.2 41.1 reduce-scatter.43
where the time goes:
time: 1770 us; the launch traced here: 1750 us
  waiting for transfers between devices  662 us (37%)
  matrix products  404 us (23%)
  local copies, waits for them, and re-layouts  376 us (21%)
  other arithmetic  151 us (9%)
  blocking collectives  127 us (7%)
  between operations  22.5 us (1%)
    squeeze x112, local copies, waits for them, and re-layouts, delta_rule(): lax.scan(jax.checkpoint(advance), initial, (weighted_keys, weighted_value...  150 us
    dot_general x64, matrix products, advance(): jnp.einsum('hid,hvd->hiv', w_keys, state, precision=lax.Precision.HIGHEST)  79.3 us
    dot_general x48, matrix products, advance(): jnp.einsum('hjv,jhd->hvd', update * block_tail[..., None], block_keys, pr...  69.5 us
    unnamed x32, waiting for transfers between devices  69 us
    dot_general x48, matrix products, advance(): jnp.einsum('hij,hjv->ihv', block_scores, update, precision=lax.Precision....  58.1 us
    dot_general x30, matrix products, batched(): jnp.einsum('...ij,...jk->...ik', left, right, precision=lax.Precision.HIG...  57.6 us
    unnamed x4, blocking collectives  46.3 us
    all_gather x1, waiting for transfers between devices, body(): lax.all_gather(grad_out.astype(jnp.bfloat16), 'tp', axis=0, tiled=True)  46 us
  transfers between devices with their start and end apart: 27, of which 18 were waited for; matrix products, arithmetic and copies ran while one was open for 52% of the time, Pallas kernels for 0%

commit v1 on v0

v1 whole, which is shorter than its diff:
```python
import functools
import jax
import jax.numpy as jnp
from jax import lax
from jax.experimental import pallas as pl
from jax.experimental.pallas import tpu as pltpu
from jax.sharding import PartitionSpec as P

epsilon = 1e-06
CHUNK = 128
F32 = jnp.float32
BF16 = jnp.bfloat16
NN = (((1,), (0,)), ((), ()))
NT = (((1,), (1,)), ((), ()))
TN = (((0,), (0,)), ((), ()))


def mm(left, right, dims=NN):
    return lax.dot_general(left.astype(BF16), right.astype(BF16), dims, preferred_element_type=F32)


def mm_exact(left, right, dims=NN):
    return lax.dot_general(left, right, dims, precision=lax.Precision.HIGHEST, preferred_element_type=F32)


def sigmoid(x):
    return 1.0 / (1.0 + jnp.exp(-x))


def softplus(x):
    return jnp.maximum(x, 0.0) + jnp.log1p(jnp.exp(-jnp.abs(x)))


def grid_index(shape, axis):
    return lax.broadcasted_iota(jnp.int32, shape, axis)


def unit_inverse(system):
    size = system.shape[0]
    row = grid_index(system.shape, 0)
    col = grid_index(system.shape, 1)
    near = (row // 2) == (col // 2)
    result = jnp.where(row == col, 1.0, 0.0) - jnp.where(near, system, 0.0)
    width = 2
    while width < size:
        joined = (row // (2 * width)) == (col // (2 * width))
        apart = (row // width) != (col // width)
        off = jnp.where(joined & apart, system, 0.0)
        result = result - mm(mm(result, off), result)
        width *= 2
    return result


def rows_ext(ext_ref, offset, rows):
    return ext_ref[pl.ds(offset, rows), :]


def conv_rows(ext_ref, taps_ref, rows):
    total = taps_ref[0:1, :] * ext_ref[pl.ds(8, rows), :]
    for offset in range(1, 4):
        total = total + taps_ref[offset : offset + 1, :] * ext_ref[pl.ds(8 - offset, rows), :]
    return total


def unit_rows(values, scale):
    factor = lax.rsqrt(jnp.sum(values * values, axis=-1, keepdims=True) + epsilon)
    return values * factor * scale, factor


def logits_act(logits, misc_ref, heads):
    lane = grid_index(logits.shape, 1)
    decay = misc_ref[0:1, :] * softplus(logits + misc_ref[1:2, :])
    return jnp.where(lane < heads, sigmoid(logits), decay)


def decay_tables(act, heads):
    rows = act.shape[0]
    row = grid_index((rows, rows), 0)
    col = grid_index((rows, rows), 1)
    tri = jnp.where(row >= col, 1.0, 0.0)
    total = mm_exact(tri, act)
    return total, jnp.transpose(total)


MESH = pl.DeviceIdType.MESH


def cost(micros):
    return pl.CostEstimate(flops=0, bytes_accessed=micros * 3000000, transcendentals=0)


def line_barrier(me, size):
    barrier = pltpu.get_barrier_semaphore()

    @pl.when(me > 0)
    def _():
        pl.semaphore_signal(barrier, inc=1, device_id={"tp": me - 1}, device_id_type=MESH)

    @pl.when(me < size - 1)
    def _():
        pl.semaphore_signal(barrier, inc=1, device_id={"tp": me + 1}, device_id_type=MESH)

    pl.semaphore_wait(barrier, jnp.where(me > 0, 1, 0) + jnp.where(me < size - 1, 1, 0))


PIECE = 32


class StreamSum:
    def __init__(self, size, lag, blocks, x_ref, sum_ref, from_left, from_right, to_left, to_right, sl, sr, rl, rr):
        self.size, self.lag, self.blocks = size, lag, blocks
        self.me = lax.axis_index("tp")
        self.x, self.sum = x_ref, sum_ref
        self.from_left, self.from_right, self.to_left, self.to_right = from_left, from_right, to_left, to_right
        self.sl, self.sr, self.rl, self.rr = sl, sr, rl, rr
        self.half = CHUNK // 2 // PIECE
        self.halves = x_ref.shape[0] // (CHUNK // 2)

    def part(self, ref, p):
        return ref.at[pl.ds(pl.multiple_of(p * PIECE, PIECE), PIECE), :]

    def right(self, src, p):
        return pltpu.make_async_remote_copy(
            src_ref=self.part(src, p), dst_ref=self.part(self.from_left, p), send_sem=self.sr.at[p], recv_sem=self.rl.at[p],
            device_id={"tp": jnp.minimum(self.me + 1, self.size - 1)}, device_id_type=MESH)

    def left(self, src, p):
        return pltpu.make_async_remote_copy(
            src_ref=self.part(src, p), dst_ref=self.part(self.from_right, p), send_sem=self.sl.at[p], recv_sem=self.rr.at[p],
            device_id={"tp": jnp.maximum(self.me - 1, 0)}, device_id_type=MESH)

    def order(self, half):
        return half

    def send_own(self, step):
        @pl.when(self.me == 0)
        def _():
            @pl.loop(0, 2 * self.half)
            def _(k):
                self.right(self.x, self.order(2 * step) * self.half + k).start()

        @pl.when(self.me == self.size - 1)
        def _():
            @pl.loop(0, 2 * self.half)
            def _(k):
                self.left(self.x, self.order(2 * step) * self.half + k).start()

    def advance(self, tick):
        me, size, halves = self.me, self.size, self.halves
        hr = tick - 1 - self.lag * me
        hl = tick - 1 - self.lag * (size - 1 - me)
        hf = tick - 1 - self.lag * jnp.maximum(me, size - 1 - me)

        @pl.loop(0, self.half)
        def _(k):
            @pl.when((me > 0) & (hr >= 0) & (hr < halves))
            def _():
                p = hr * self.half + k
                self.right(self.to_right, p).wait_recv()

                @pl.when(me < size - 1)
                def _():
                    self.part(self.to_right, p)[...] = (
                        self.part(self.from_left, p)[...].astype(F32) + self.part(self.x, p)[...].astype(F32)).astype(BF16)
                    self.right(self.to_right, p).start()

            @pl.when((me < size - 1) & (hl >= 0) & (hl < halves))
            def _():
                p = hl * self.half + k
                self.left(self.to_left, p).wait_recv()

                @pl.when(me > 0)
                def _():
                    self.part(self.to_left, p)[...] = (
                        self.part(self.from_right, p)[...].astype(F32) + self.part(self.x, p)[...].astype(F32)).astype(BF16)
                    self.left(self.to_left, p).start()

            @pl.when((hf >= 0) & (hf < halves))
            def _():
                p = hf * self.half + k
                own = self.part(self.x, p)[...].astype(F32)

                @pl.when(me == 0)
                def _():
                    self.part(self.sum, p)[...] = own + self.part(self.from_right, p)[...].astype(F32)

                @pl.when(me == size - 1)
                def _():
                    self.part(self.sum, p)[...] = own + self.part(self.from_left, p)[...].astype(F32)

                @pl.when((me > 0) & (me < size - 1))
                def _():
                    self.part(self.sum, p)[...] = (
                        own + self.part(self.from_left, p)[...].astype(F32) + self.part(self.from_right, p)[...].astype(F32))

    def finish(self, step):
        @pl.when(step == self.blocks - 1)
        def _():
            @pl.loop(self.halves, self.halves + 1 + self.lag * (self.size - 1))
            def _(tick):
                self.advance(tick)

            @pl.loop(0, self.halves * self.half)
            def _(p):
                @pl.when(self.me < self.size - 1)
                def _():
                    self.right(self.to_right, p).wait_send()

                @pl.when(self.me > 0)
                def _():
                    self.left(self.to_left, p).wait_send()


def stream_scratch(rows, width):
    buf = pltpu.VMEM((rows, width), BF16)
    dma = pltpu.SemaphoreType.DMA((rows // PIECE,))
    return [buf, buf, buf, buf, buf, dma, dma, dma, dma]


def fwd_kernel(
    size, lag, heads, dk, dv, proj_ref, taps_ref, misc_ref, gain_ref, out_w_ref, gated_ref, mixed_ref, u_ref, inv_ref, start_ref, sum_ref,
    ext_ref, state_ref, x_ref, *line_refs
):
    rows = CHUNK
    step = pl.program_id(0)
    line = StreamSum(size, lag, pl.num_programs(0), x_ref, sum_ref, *line_refs)
    kw, vw = heads * dk, heads * dv
    conv_w = 2 * kw + vw

    @pl.when(step == 0)
    def _():
        line_barrier(line.me, size)
        ext_ref[0:8, :] = jnp.zeros((8, conv_w), F32)
        state_ref[...] = jnp.zeros_like(state_ref)

    ext_ref[pl.ds(8, rows), :] = proj_ref[:, 0:conv_w]
    conv = conv_rows(ext_ref, taps_ref, rows)
    ext_ref[0:8, :] = ext_ref[pl.ds(rows, 8), :]
    act = conv * sigmoid(conv)
    logits = logits_act(proj_ref[:, conv_w + vw :], misc_ref, heads)
    cum, cum_t = decay_tables(logits, heads)
    row = grid_index((rows, rows), 0)
    col = grid_index((rows, rows), 1)
    for h in range(heads):
        q, _ = unit_rows(act[:, h * dk : (h + 1) * dk], dk ** (-0.5))
        k, _ = unit_rows(act[:, kw + h * dk : kw + (h + 1) * dk], 1.0)
        v = act[:, 2 * kw + h * dv : 2 * kw + (h + 1) * dv].astype(BF16).astype(F32)
        q, k = q.astype(BF16), k.astype(BF16)
        beta = logits[:, h : h + 1]
        g_col = cum[:, heads + h : heads + h + 1]
        g_row = cum_t[heads + h : heads + h + 1, :]
        decay = jnp.where(row >= col, jnp.exp(jnp.where(row >= col, g_col - g_row, 0.0)), 0.0)
        grams = mm(jnp.concatenate([k, q], axis=0), k, NT)
        system = jnp.where(row > col, decay * grams[:rows], 0.0) * beta
        scores = decay * grams[rows:]
        inverse = unit_inverse(system)
        growth = jnp.exp(g_col)
        g_last = g_row[:, rows - 1 : rows]
        tail = jnp.exp(g_last - g_col)
        state = state_ref[:, h * dv : (h + 1) * dv]
        start_ref[0, :, h * dv : (h + 1) * dv] = state.astype(start_ref.dtype)
        seen = mm(jnp.concatenate([k, q], axis=0), state)
        u = mm(inverse, beta * (v - growth * seen[:rows]))
        mixed = growth * seen[rows:] + mm(scores, u)
        state_ref[:, h * dv : (h + 1) * dv] = jnp.exp(g_last) * state + mm(k, tail * u, TN)
        cols = slice(h * dv, (h + 1) * dv)
        mixed_ref[:, cols] = mixed
        u_ref[:, cols] = u.astype(u_ref.dtype)
        inv_ref[:, h * rows : (h + 1) * rows] = inverse.astype(inv_ref.dtype)
        gate = proj_ref[:, conv_w + h * dv : conv_w + (h + 1) * dv]
        scale = lax.rsqrt(jnp.mean(mixed * mixed, axis=-1, keepdims=True) + epsilon)
        gated = (mixed * scale * gain_ref[:, cols] * gate * sigmoid(gate)).astype(BF16)
        gated_ref[:, cols] = gated
        part = mm(gated, out_w_ref[conv_w + vw + 128 + h * dv : conv_w + vw + 128 + (h + 1) * dv, :])
        branch = part if h == 0 else branch + part
        if h == 0:
            line.advance(2 * step)
    x_ref[pl.ds(pl.multiple_of(step * rows, rows), rows), :] = branch.astype(BF16)
    line.send_own(step)
    line.advance(2 * step + 1)
    line.finish(step)


def mixer_fwd(proj, taps, misc, gain, out_w, heads, dk, dv, size, lag, collective_id):
    total_rows, width = proj.shape
    chunks = total_rows // CHUNK
    vw = heads * dv
    conv_w = 2 * heads * dk + vw
    model = out_w.shape[1]
    blk = lambda w: pl.BlockSpec((CHUNK, w), lambda c: (c, 0))
    full = lambda a: pl.BlockSpec(a.shape, lambda c: (0, 0))
    return pl.pallas_call(
        functools.partial(fwd_kernel, size, lag, heads, dk, dv),
        grid=(chunks,),
        in_specs=[blk(width), full(taps), full(misc), full(gain), full(out_w)],
        out_specs=[
            blk(vw), blk(vw), blk(vw), blk(heads * CHUNK), pl.BlockSpec((1, dk, vw), lambda c: (c, 0, 0)),
            pl.BlockSpec((total_rows, model), lambda c: (0, 0)),
        ],
        out_shape=[
            jax.ShapeDtypeStruct((total_rows, vw), BF16),
            jax.ShapeDtypeStruct((total_rows, vw), F32),
            jax.ShapeDtypeStruct((total_rows, vw), BF16),
            jax.ShapeDtypeStruct((total_rows, heads * CHUNK), BF16),
            jax.ShapeDtypeStruct((chunks, dk, vw), BF16),
            jax.ShapeDtypeStruct((total_rows, model), F32),
        ],
        scratch_shapes=[pltpu.VMEM((8 + CHUNK, conv_w), F32), pltpu.VMEM((dk, vw), F32)] + stream_scratch(total_rows, model),
        compiler_params=pltpu.CompilerParams(collective_id=collective_id, has_side_effects=True),
        cost_estimate=cost(65),
        name="mixer_fwd",
    )(proj, taps, misc, gain, out_w)


def bwd_kernel(heads, dk, dv, grad_ref, proj_ref, before_ref, taps_ref, misc_ref, gain_ref, mixed_ref, u_ref, inv_ref, start_ref,
               gproj_ref, tapg_ref, small_ref, gaing_ref, ext_ref, back_ref, dstate_ref):
    rows = CHUNK
    kw, vw = heads * dk, heads * dv
    conv_w = 2 * kw + vw
    step = pl.program_id(0)
    chunk = pl.num_programs(0) - 1 - step

    @pl.when(step == 0)
    def _():
        back_ref[pl.ds(rows, 8), :] = jnp.zeros((8, conv_w), F32)
        dstate_ref[...] = jnp.zeros_like(dstate_ref)
        tapg_ref[...] = jnp.zeros_like(tapg_ref)
        small_ref[...] = jnp.zeros_like(small_ref)
        gaing_ref[...] = jnp.zeros_like(gaing_ref)

    ext_ref[0:8, :] = jnp.where(chunk > 0, before_ref[:, 0:conv_w], 0.0)
    ext_ref[pl.ds(8, rows), :] = proj_ref[:, 0:conv_w]
    conv = conv_rows(ext_ref, taps_ref, rows)
    sig = sigmoid(conv)
    act = conv * sig
    dact = sig * (1.0 + conv * (1.0 - sig))
    raw = proj_ref[:, conv_w + vw :]
    logits = logits_act(raw, misc_ref, heads)
    cum, cum_t = decay_tables(logits, heads)
    row = grid_index((rows, rows), 0)
    col = grid_index((rows, rows), 1)
    lane = col
    dlog = jnp.zeros((rows, rows), F32)
    for h in range(heads):
        cols = slice(h * dv, (h + 1) * dv)
        gate = proj_ref[:, conv_w + h * dv : conv_w + (h + 1) * dv]
        gsig = sigmoid(gate)
        mixed = mixed_ref[:, cols]
        grad = grad_ref[:, cols].astype(F32)
        gain = gain_ref[:, cols]
        scale = lax.rsqrt(jnp.mean(mixed * mixed, axis=-1, keepdims=True) + epsilon)
        unit = mixed * scale
        weighted = grad * gate * gsig
        gaing_ref[0:1, cols] += jnp.sum(weighted * unit, axis=0, keepdims=True)
        gproj_ref[:, conv_w + h * dv : conv_w + (h + 1) * dv] = (grad * gain * unit * gsig * (1.0 + gate * (1.0 - gsig))).astype(BF16)
        pulled = weighted * gain
        d_out = scale * (pulled - unit * jnp.mean(pulled * unit, axis=-1, keepdims=True))
        qs, ks = slice(h * dk, (h + 1) * dk), slice(kw + h * dk, kw + (h + 1) * dk)
        vs = slice(2 * kw + h * dv, 2 * kw + (h + 1) * dv)
        q_f, q_scale = unit_rows(act[:, qs], dk ** (-0.5))
        k_f, k_scale = unit_rows(act[:, ks], 1.0)
        v = act[:, vs].astype(BF16).astype(F32)
        q, k = q_f.astype(BF16), k_f.astype(BF16)
        q32, k32 = q.astype(F32), k.astype(F32)
        beta = logits[:, h : h + 1]
        g_col = cum[:, heads + h : heads + h + 1]
        g_row = cum_t[heads + h : heads + h + 1, :]
        decay = jnp.where(row >= col, jnp.exp(jnp.where(row >= col, g_col - g_row, 0.0)), 0.0)
        grams = mm(jnp.concatenate([k, q], axis=0), k, NT)
        plain = jnp.where(row > col, decay * grams[:rows], 0.0)
        scores = decay * grams[rows:]
        growth = jnp.exp(g_col)
        g_last = g_row[:, rows - 1 : rows]
        tail = jnp.exp(g_last - g_col)
        inverse = inv_ref[:, h * rows : (h + 1) * rows]
        u = u_ref[:, cols]
        start = start_ref[0, :, cols]
        d_end = dstate_ref[:, cols]
        d_end_b = d_end.astype(BF16)
        d_u = mm(scores, d_out, TN) + tail * mm(k, d_end_b)
        d_rhs = mm(inverse, d_u, TN)
        d_seen = -growth * d_rhs
        g_out = growth * d_out
        both = mm(jnp.concatenate([d_rhs, d_out], axis=0), u, NT)
        d_sys = jnp.where(row > col, -both[:rows], 0.0)
        d_scores = jnp.where(row >= col, both[rows:], 0.0)
        dstate_ref[:, cols] = jnp.exp(g_last) * d_end + mm(jnp.concatenate([k, q], axis=0), jnp.concatenate([beta * d_seen, g_out], axis=0), TN)
        pull = mm(jnp.concatenate([d_seen, g_out], axis=0), start, NT)
        d_k_seen, d_q1 = pull[:rows], pull[rows:]
        d_k_tail = tail * mm(u, d_end_b, NT)
        d_qk = d_scores * decay
        d_gram = d_sys * decay * beta
        d_gram = d_gram + jnp.transpose(d_gram)
        near = mm(jnp.concatenate([d_qk, d_gram], axis=0), k)
        d_q = d_q1 + near[:rows]
        d_k = beta * d_k_seen + d_k_tail + near[rows:] + mm(d_qk, q, TN)
        d_v = beta * d_rhs
        seen_dot = jnp.sum(k32 * d_k_seen, axis=-1, keepdims=True)
        tail_dot = jnp.sum(k32 * d_k_tail, axis=-1, keepdims=True)
        sys_plain = d_sys * plain
        d_beta = jnp.sum(sys_plain, axis=-1, keepdims=True) + jnp.sum(d_rhs * v, axis=-1, keepdims=True) + seen_dot
        mixed_terms = sys_plain * beta + d_scores * scores
        d_cum = (
            jnp.sum(mixed_terms, axis=-1, keepdims=True)
            - jnp.sum(jnp.transpose(mixed_terms), axis=-1, keepdims=True)
            + beta * seen_dot
            - tail_dot
            + jnp.sum(q32 * d_q1, axis=-1, keepdims=True)
        )
        d_last = jnp.sum(tail_dot, axis=0, keepdims=True) + jnp.exp(g_last) * jnp.sum(
            jnp.sum(d_end * start.astype(F32), axis=-1, keepdims=True), axis=0, keepdims=True
        )
        d_cum = d_cum + jnp.where(grid_index((rows, 1), 0) == rows - 1, d_last, 0.0)
        dlog = jnp.where(lane == h, d_beta, jnp.where(lane == heads + h, d_cum, dlog))
        q_hat, k_hat = q_f * dk**0.5, k_f
        d_q = d_q * dk ** (-0.5)
        d_qa = q_scale * (d_q - q_hat * jnp.sum(d_q * q_hat, axis=-1, keepdims=True))
        d_ka = k_scale * (d_k - k_hat * jnp.sum(d_k * k_hat, axis=-1, keepdims=True))
        back_ref[0:rows, qs] = d_qa * dact[:, qs]
        back_ref[0:rows, ks] = d_ka * dact[:, ks]
        back_ref[0:rows, vs] = d_v * dact[:, vs]
    tri = jnp.where(row <= col, 1.0, 0.0)
    d_decay = mm_exact(tri, dlog)
    shifted = sigmoid(raw + misc_ref[1:2, :])
    d_raw = jnp.where(lane < heads, dlog * logits * (1.0 - logits), d_decay * misc_ref[0:1, :] * shifted)
    d_raw = jnp.where(lane < 2 * heads, d_raw, 0.0)
    gproj_ref[:, conv_w + vw :] = d_raw.astype(BF16)
    small_ref[0:1, :] += jnp.sum(d_decay * logits, axis=0, keepdims=True)
    small_ref[1:2, :] += jnp.sum(d_raw, axis=0, keepdims=True)
    here = back_ref[0:rows, :]
    total = taps_ref[0:1, :] * here
    tapg_ref[0:1, :] += jnp.sum(here * ext_ref[pl.ds(8, rows), :], axis=0, keepdims=True)
    for offset in range(1, 4):
        total = total + taps_ref[offset : offset + 1, :] * back_ref[pl.ds(offset, rows), :]
        tapg_ref[offset : offset + 1, :] += jnp.sum(here * ext_ref[pl.ds(8 - offset, rows), :], axis=0, keepdims=True)
    gproj_ref[:, 0:conv_w] = total.astype(BF16)
    back_ref[pl.ds(rows, 8), :] = back_ref[0:8, :]


def mixer_bwd(grad, proj, taps, misc, gain, mixed, u, inverse, start, heads, dk, dv):
    total_rows, width = proj.shape
    chunks = total_rows // CHUNK
    conv_w = 2 * heads * dk + heads * dv
    vw = heads * dv
    last = chunks - 1
    blk = lambda w: pl.BlockSpec((CHUNK, w), lambda c: (last - c, 0))
    full = lambda a: pl.BlockSpec(a.shape, lambda c: (0, 0))
    per = CHUNK // 8
    return pl.pallas_call(
        functools.partial(bwd_kernel, heads, dk, dv),
        grid=(chunks,),
        in_specs=[
            blk(vw), blk(width),
            pl.BlockSpec((8, width), lambda c: (jnp.maximum((last - c) * per - 1, 0), 0)),
            full(taps), full(misc), full(gain), blk(vw), blk(vw), blk(heads * CHUNK),
            pl.BlockSpec((1, dk, vw), lambda c: (last - c, 0, 0)),
        ],
        out_specs=[
            blk(width),
            pl.BlockSpec((8, conv_w), lambda c: (0, 0)),
            pl.BlockSpec((8, 128), lambda c: (0, 0)),
            pl.BlockSpec((8, vw), lambda c: (0, 0)),
        ],
        out_shape=[
            jax.ShapeDtypeStruct((total_rows, width), BF16),
            jax.ShapeDtypeStruct((8, conv_w), F32),
            jax.ShapeDtypeStruct((8, 128), F32),
            jax.ShapeDtypeStruct((8, vw), F32),
        ],
        scratch_shapes=[
            pltpu.VMEM((8 + CHUNK, conv_w), F32),
            pltpu.VMEM((CHUNK + 8, conv_w), F32),
            pltpu.VMEM((dk, vw), F32),
        ],
        cost_estimate=cost(27),
        name="mixer_bwd",
    )(grad, proj, proj, taps, misc, gain, mixed, u, inverse, start)


def ff_kernel(
    size, lag, wide, tokens_ref, branch_ref, grad_ref, gain_ref, w_ref, normed_ref, inner_ref, acts_ref, part_ref, gaing_ref, sum_ref, x_ref, *line_refs
):
    rows = CHUNK
    step = pl.program_id(0)
    line = StreamSum(size, lag, pl.num_programs(0), x_ref, sum_ref, *line_refs)

    @pl.when(step == 0)
    def _():
        line_barrier(line.me, size)
        gaing_ref[...] = jnp.zeros_like(gaing_ref)

    hidden = (tokens_ref[...].astype(F32) + branch_ref[...]).astype(BF16).astype(F32)
    scale = lax.rsqrt(jnp.mean(hidden * hidden, axis=-1, keepdims=True) + epsilon)
    unit = hidden * scale
    normed = (unit * gain_ref[...]).astype(BF16)
    normed_ref[...] = normed
    gate = mm(normed, w_ref[0:wide, :], NT)
    up = mm(normed, w_ref[wide : 2 * wide, :], NT)
    sig = sigmoid(gate)
    inner = (gate * sig * up).astype(BF16)
    inner_ref[...] = inner
    part_ref[...] = mm(inner, w_ref[2 * wide : 3 * wide, :]).astype(BF16)
    line.advance(2 * step)
    grad_inner = mm(grad_ref[...], w_ref[2 * wide : 3 * wide, :], NT)
    grad_gate = (grad_inner * up * sig * (1.0 + gate * (1.0 - sig))).astype(BF16)
    grad_up = (grad_inner * gate * sig).astype(BF16)
    acts_ref[:, 0:wide] = grad_gate
    acts_ref[:, wide : 2 * wide] = grad_up
    grad_normed = mm(grad_gate, w_ref[0:wide, :]) + mm(grad_up, w_ref[wide : 2 * wide, :])
    gaing_ref[0:1, :] += jnp.sum(grad_normed * unit, axis=0, keepdims=True)
    pulled = grad_normed * gain_ref[...]
    sent = scale * (pulled - unit * jnp.mean(pulled * unit, axis=-1, keepdims=True))
    x_ref[pl.ds(pl.multiple_of(step * rows, rows), rows), :] = sent.astype(BF16)
    line.send_own(step)
    line.advance(2 * step + 1)
    line.finish(step)


def feed_forward(tokens, branch, grad, gain, w_rows, wide, size, lag, collective_id):
    total_rows, model = tokens.shape
    chunks = total_rows // CHUNK
    blk = lambda w: pl.BlockSpec((CHUNK, w), lambda c: (c, 0))
    full = lambda r, w: pl.BlockSpec((r, w), lambda c: (0, 0))
    return pl.pallas_call(
        functools.partial(ff_kernel, size, lag, wide),
        grid=(chunks,),
        in_specs=[blk(model), blk(model), blk(model), full(1, model), full(3 * wide, model)],
        out_specs=[blk(model), blk(wide), blk(2 * wide), blk(model), full(8, model), full(total_rows, model)],
        out_shape=[
            jax.ShapeDtypeStruct((total_rows, model), BF16),
            jax.ShapeDtypeStruct((total_rows, wide), BF16),
            jax.ShapeDtypeStruct((total_rows, 2 * wide), BF16),
            jax.ShapeDtypeStruct((total_rows, model), BF16),
            jax.ShapeDtypeStruct((8, model), F32),
            jax.ShapeDtypeStruct((total_rows, model), F32),
        ],
        scratch_shapes=stream_scratch(total_rows, model),
        compiler_params=pltpu.CompilerParams(collective_id=collective_id, has_side_effects=True),
        cost_estimate=cost(65),
        name="feed_forward",
    )(tokens, branch, grad, gain, w_rows)


def peer_barrier(fsdp, tp):
    me_f, me_t = lax.axis_index("fsdp"), lax.axis_index("tp")
    barrier = pltpu.get_barrier_semaphore()

    @pl.loop(1, fsdp)
    def _(d):
        pl.semaphore_signal(barrier, inc=1, device_id={"fsdp": (me_f + d) % fsdp}, device_id_type=MESH)

    @pl.loop(1, tp)
    def _(d):
        pl.semaphore_signal(barrier, inc=1, device_id={"tp": (me_t + d) % tp}, device_id_type=MESH)

    pl.semaphore_wait(barrier, fsdp + tp - 2)


def line_gather_kernel(fsdp, size, pieces, x_ref, tile_ref, out_ref, tiles_ref, own_sem, sl, sr, rl, rr, sp, rp, st, rt):
    me = lax.axis_index("tp")
    shard = x_ref.shape[0]
    rows = shard // pieces
    own = pltpu.make_async_copy(x_ref, out_ref.at[pl.ds(pl.multiple_of(me * shard, shard), shard), :], own_sem)
    own.start()
    me_f = lax.axis_index("fsdp")
    tiles_ref[pl.ds(me_f, 1), pl.ds(me, 1)] = tile_ref[...][None, None]
    peer_barrier(fsdp, size)

    def along(d, slot):
        return pltpu.make_async_remote_copy(
            src_ref=tile_ref, dst_ref=tiles_ref.at[me_f, slot], send_sem=st.at[d], recv_sem=rt.at[slot],
            device_id={"tp": (me + d) % size}, device_id_type=MESH)

    def across(d, slot):
        return pltpu.make_async_remote_copy(
            src_ref=tiles_ref.at[me_f], dst_ref=tiles_ref.at[slot], send_sem=sp.at[d], recv_sem=rp.at[slot],
            device_id={"fsdp": (me_f + d) % fsdp}, device_id_type=MESH)

    @pl.loop(1, size)
    def _(d):
        along(d, me).start()

    def region(ref, s, k):
        return ref.at[pl.ds(pl.multiple_of(s * shard + k * rows, rows), rows), :]

    def to_right(src, s, k):
        return pltpu.make_async_remote_copy(
            src_ref=src, dst_ref=region(out_ref, s, k), send_sem=sr.at[s * pieces + k], recv_sem=rl.at[s * pieces + k],
            device_id={"tp": jnp.minimum(me + 1, size - 1)}, device_id_type=MESH)

    def to_left(src, s, k):
        return pltpu.make_async_remote_copy(
            src_ref=src, dst_ref=region(out_ref, s, k), send_sem=sl.at[s * pieces + k], recv_sem=rr.at[s * pieces + k],
            device_id={"tp": jnp.maximum(me - 1, 0)}, device_id_type=MESH)

    for k in range(pieces):
        src = x_ref.at[pl.ds(k * rows, rows), :]

        @pl.when(me < size - 1)
        def _():
            to_right(src, me, k).start()

        @pl.when(me > 0)
        def _():
            to_left(src, me, k).start()

    @pl.loop(1, size)
    def _(d):
        along(d, (me + d) % size).wait_recv()

    @pl.loop(1, fsdp)
    def _(d):
        across(d, me_f).start()

    @pl.loop(0, (size - 1) * pieces)
    def _(t):
        d = t // pieces + 1
        k = t % pieces
        s_left, s_right = me - d, me + d

        @pl.when(s_left >= 0)
        def _():
            to_right(region(out_ref, s_left, k), s_left, k).wait_recv()

            @pl.when(me < size - 1)
            def _():
                to_right(region(out_ref, s_left, k), s_left, k).start()

        @pl.when(s_right < size)
        def _():
            to_left(region(out_ref, s_right, k), s_right, k).wait_recv()

            @pl.when(me > 0)
            def _():
                to_left(region(out_ref, s_right, k), s_right, k).start()

    own.wait()

    @pl.loop(1, fsdp)
    def _(d):
        across(d, (me_f + d) % fsdp).wait_recv()

    @pl.loop(1, size)
    def _(d):
        along(d, me).wait_send()

    @pl.loop(1, fsdp)
    def _(d):
        across(d, me_f).wait_send()

    @pl.loop(0, size * pieces)
    def _(t):
        s, k = t // pieces, t % pieces

        @pl.when((me < size - 1) & (s <= me))
        def _():
            to_right(region(out_ref, s, k), s, k).wait_send()

        @pl.when((me > 0) & (s >= me))
        def _():
            to_left(region(out_ref, s, k), s, k).wait_send()


def line_gather(x, tile, fsdp, size, pieces, collective_id):
    vm = pl.BlockSpec(memory_space=pltpu.VMEM)
    dma = pltpu.SemaphoreType.DMA((size * pieces,))
    plane, line = pltpu.SemaphoreType.DMA((fsdp,)), pltpu.SemaphoreType.DMA((size,))
    return pl.pallas_call(
        functools.partial(line_gather_kernel, fsdp, size, pieces),
        out_shape=[
            jax.ShapeDtypeStruct((size * x.shape[0], x.shape[1]), x.dtype),
            jax.ShapeDtypeStruct((fsdp, size) + tile.shape, tile.dtype),
        ],
        in_specs=[vm, vm], out_specs=[vm, vm],
        scratch_shapes=[pltpu.SemaphoreType.DMA, dma, dma, dma, dma, plane, plane, line, line],
        compiler_params=pltpu.CompilerParams(collective_id=collective_id, has_side_effects=True),
        cost_estimate=cost(40),
        name="line_gather",
    )(x, tile)


class PlaneSum:
    def __init__(self, n, order, cols, src_ref, out_ref, acc_ref, recv_ref, send_sem, recv_sem):
        self.n, self.order, self.cols = n, order, cols
        self.stages = len(order)
        self.me = lax.axis_index("fsdp")
        self.block = src_ref.shape[0] // n
        self.src, self.out, self.acc, self.recv = src_ref, out_ref, acc_ref, recv_ref
        self.send_sem, self.recv_sem = send_sem, recv_sem

    def bit(self, b):
        return (self.me // b) % 2

    def owner(self, stage, i, flip):
        total = 0
        for b in self.order[:stage]:
            total = total + self.bit(b) * b
        b = self.order[stage]
        total = total + ((1 - self.bit(b)) if flip else self.bit(b)) * b
        for j, r in enumerate(self.order[stage + 1 :]):
            total = total + ((i // (2**j)) % 2) * r
        return total

    def place(self, pair):
        total = 0
        for j, r in enumerate(self.order[1:]):
            total = total + ((pair // (r // 2)) % 2) * 2**j
        return total

    def rows(self, g):
        return pl.ds(pl.multiple_of(g * self.block, self.block), self.block)

    def copy(self, stage, i):
        b = self.order[stage]
        src = self.src if stage == 0 else self.acc
        slot = self.n - (self.n >> stage) + i
        return pltpu.make_async_remote_copy(
            src_ref=src.at[self.rows(self.owner(stage, i, True)), self.cols], dst_ref=self.recv.at[self.rows(slot), self.cols],
            send_sem=self.send_sem.at[slot], recv_sem=self.recv_sem.at[slot],
            device_id={"fsdp": self.me + b - 2 * b * self.bit(b)}, device_id_type=MESH)

    def total(self, stage, i):
        self.copy(stage, i).wait_recv()
        g = self.owner(stage, i, False)
        slot = self.n - (self.n >> stage) + i
        src = self.src if stage == 0 else self.acc
        return g, src[self.rows(g), self.cols].astype(F32) + self.recv[self.rows(slot), self.cols].astype(F32)

    def advance(self, stage):
        if stage == self.stages - 1:
            _, total = self.total(stage, 0)
            self.out[:, self.cols] = total
            return
        mine = self.bit(self.order[stage + 1])
        for flip in (True, False):
            @pl.loop(0, self.n >> (stage + 2))
            def _(i):
                g, total = self.total(stage, 2 * i + (1 - mine if flip else mine))
                self.acc[self.rows(g), self.cols] = total.astype(BF16)
                if flip:
                    self.copy(stage + 1, i).start()

    def finish(self):
        @pl.loop(0, self.n // 2)
        def _(i):
            self.copy(0, i).wait_send()

        for stage in range(1, self.stages):
            @pl.loop(0, self.n >> (stage + 1))
            def _(i):
                self.copy(stage, i).wait_send()


def halving_orders(n):
    bits = [2**j for j in range(n.bit_length() - 1)]
    return bits, bits[:1] + bits[:0:-1]


def last_kernel(
    fsdp, size, pieces, slack, gproj_ref, w_ref, normed_ref, tokens_ref, gain_ref, gbranch_ref, gated_ref, base_ref, small_ref, tapg_ref,
    out_ref, small_out, tap_out, shard_ref,
    x_ref, grads, acc, recv, small, small_in, small_line, tap_in, from_left, from_right, to_left, to_right,
    sl, sr, rl, rr, sp, rp, st, rt, sk, rk, sa, ra, sb, rb
):
    me, me_f = lax.axis_index("tp"), lax.axis_index("fsdp")
    shard = x_ref.shape[0] // size
    rows = shard // pieces
    count = (size - 1) * pieces
    proj_w = gproj_ref.shape[1]
    peer_barrier(fsdp, size)

    def across(d, slot):
        return pltpu.make_async_remote_copy(
            src_ref=small, dst_ref=small_in.at[slot], send_sem=sp.at[d], recv_sem=rp.at[slot],
            device_id={"fsdp": (me_f + d) % fsdp}, device_id_type=MESH)

    def taps_across(d, slot):
        return pltpu.make_async_remote_copy(
            src_ref=tapg_ref, dst_ref=tap_in.at[slot], send_sem=sk.at[d], recv_sem=rk.at[slot],
            device_id={"fsdp": (me_f + d) % fsdp}, device_id_type=MESH)

    def along(d, slot):
        return pltpu.make_async_remote_copy(
            src_ref=small_out, dst_ref=small_line.at[slot], send_sem=st.at[d], recv_sem=rt.at[slot],
            device_id={"tp": (me + d) % size}, device_id_type=MESH)

    width = grads.shape[1]
    cut = (width // 256 + width // 128 % 2) * 128
    order_a, order_b = halving_orders(fsdp)
    planes = [
        PlaneSum(fsdp, order_a, slice(0, cut), grads, shard_ref, acc, recv, sa, ra),
        PlaneSum(fsdp, order_b, slice(cut, width), grads, shard_ref, acc, recv, sb, rb),
    ]

    def part(ref, s, k):
        return ref.at[pl.ds(pl.multiple_of(s * shard + k * rows, rows), rows), :]

    def right_copy(src, s, k):
        return pltpu.make_async_remote_copy(
            src_ref=part(src, s, k), dst_ref=part(from_left, s, k), send_sem=sr.at[s * pieces + k], recv_sem=rl.at[s * pieces + k],
            device_id={"tp": jnp.minimum(me + 1, size - 1)}, device_id_type=MESH)

    def left_copy(src, s, k):
        return pltpu.make_async_remote_copy(
            src_ref=part(src, s, k), dst_ref=part(from_right, s, k), send_sem=sl.at[s * pieces + k], recv_sem=rr.at[s * pieces + k],
            device_id={"tp": jnp.maximum(me - 1, 0)}, device_id_type=MESH)

    def exchange(t):
        ir = t - (me - 1) * slack
        il = t - (size - 2 - me) * slack
        s_r, k_r = size - 1 - ir // pieces, ir % pieces
        s_l, k_l = il // pieces, il % pieces

        @pl.when((me > 0) & (ir >= 0) & (ir < count) & (s_r >= me))
        def _():
            right_copy(to_right, s_r, k_r).wait_recv()

            @pl.when(s_r > me)
            def _():
                part(to_right, s_r, k_r)[...] = (
                    part(from_left, s_r, k_r)[...].astype(F32) + part(x_ref, s_r, k_r)[...].astype(F32)).astype(BF16)
                right_copy(to_right, s_r, k_r).start()

        @pl.when((me < size - 1) & (il >= 0) & (il < count) & (s_l <= me))
        def _():
            left_copy(to_left, s_l, k_l).wait_recv()

            @pl.when(s_l < me)
            def _():
                part(to_left, s_l, k_l)[...] = (
                    part(from_right, s_l, k_l)[...].astype(F32) + part(x_ref, s_l, k_l)[...].astype(F32)).astype(BF16)
                left_copy(to_left, s_l, k_l).start()

    small[...] = small_ref[...]

    @pl.loop(0, size)
    def _(j):
        s = (j % 2) * (j // 2) + (1 - j % 2) * (size - 1 - j // 2)
        here = pl.ds(pl.multiple_of(s * shard, shard), shard)
        grad_normed = mm(gproj_ref[here, :], w_ref[0:proj_w, :])
        values = tokens_ref[here, :].astype(F32)
        scale = lax.rsqrt(jnp.mean(values * values, axis=-1, keepdims=True) + epsilon)
        unit = values * scale
        small[0:1, :] += jnp.sum(grad_normed * unit, axis=0, keepdims=True)
        pulled = grad_normed * gain_ref[...]
        x_ref[here, :] = (scale * (pulled - unit * jnp.mean(pulled * unit, axis=-1, keepdims=True))).astype(BF16)

        @pl.when((me == 0) & (s > 0))
        def _():
            @pl.loop(0, pieces)
            def _(k):
                right_copy(x_ref, s, k).start()

        @pl.when((me == size - 1) & (s < size - 1))
        def _():
            @pl.loop(0, pieces)
            def _(k):
                left_copy(x_ref, s, k).start()

    @pl.loop(1, fsdp)
    def _(d):
        taps_across(d, me_f).start()
        across(d, me_f).start()

    block = grads.shape[0] // fsdp
    many = max(256 // block, 2)
    groups = fsdp // many
    ticks = count + (size - 2) * slack
    per = max(ticks // (3 * groups), 1)

    @pl.loop(0, groups)
    def _(i):
        here = pl.ds(pl.multiple_of(i * many * block, many * block), many * block)
        grads[here, 0:proj_w] = mm(normed_ref[here, :], gproj_ref[...]).astype(BF16)
        grads[here, proj_w:width] = mm(gbranch_ref[here, :], gated_ref[...]).astype(BF16)

        @pl.loop(0, many // 2)
        def _(m):
            for plane in planes:
                plane.copy(0, plane.place(i * (many // 2) + m)).start()

        @pl.loop(i * per, (i + 1) * per)
        def _(t):
            exchange(t)

    stages = len(order_a)
    done = groups * per
    for stage in range(stages):
        until = max(done, int(ticks * (0.4 + 0.45 * stage / max(stages - 1, 1))))

        @pl.loop(done, until)
        def _(t):
            exchange(t)

        done = until
        for plane in planes:
            plane.advance(stage)
        if stage == 0:
            small_out[...] = small[...]
            tap_out[...] = tapg_ref[...]

            @pl.loop(1, fsdp)
            def _(d):
                slot = (me_f + d) % fsdp
                across(d, slot).wait_recv()
                taps_across(d, slot).wait_recv()
                small_out[...] += small_in[pl.ds(slot, 1)][0]
                tap_out[...] += tap_in[pl.ds(slot, 1)][0]

            @pl.loop(1, size)
            def _(d):
                along(d, me).start()

    @pl.loop(done, ticks)
    def _(t):
        exchange(t)

    for plane in planes:
        plane.finish()

    @pl.loop(1, size)
    def _(d):
        along(d, me).wait_send()

    @pl.loop(1, size)
    def _(d):
        slot = (me + d) % size
        along(d, slot).wait_recv()
        small_out[...] += small_line[pl.ds(slot, 1)][0]

    @pl.loop(1, fsdp)
    def _(d):
        across(d, me_f).wait_send()
        taps_across(d, me_f).wait_send()

    @pl.loop(0, pieces)
    def _(k):
        here = pl.ds(pl.multiple_of(k * rows, rows), rows)
        total = base_ref[here, :] + part(x_ref, me, k)[...].astype(F32)

        @pl.when(me == 0)
        def _():
            out_ref[here, :] = total + part(from_right, me, k)[...].astype(F32)

        @pl.when(me == size - 1)
        def _():
            out_ref[here, :] = total + part(from_left, me, k)[...].astype(F32)

        @pl.when((me > 0) & (me < size - 1))
        def _():
            out_ref[here, :] = total + part(from_left, me, k)[...].astype(F32) + part(from_right, me, k)[...].astype(F32)

    @pl.loop(0, size * pieces)
    def _(i):
        s, k = i // pieces, i % pieces

        @pl.when(s > me)
        def _():
            right_copy(to_right, s, k).wait_send()

        @pl.when(s < me)
        def _():
            left_copy(to_left, s, k).wait_send()


def last_sums(gproj, w_rows, normed_t, tokens, gain, gbranch_t, gated, base, small, tapg, fsdp, size, pieces, slack, collective_id):
    vm = pl.BlockSpec(memory_space=pltpu.VMEM)
    total_rows, model = tokens.shape
    width = gproj.shape[1] + gated.shape[1]
    buf = pltpu.VMEM((total_rows, model), BF16)
    pack = pltpu.VMEM((model, width), BF16)
    dma = pltpu.SemaphoreType.DMA((size * pieces,))
    plane, line = pltpu.SemaphoreType.DMA((fsdp,)), pltpu.SemaphoreType.DMA((size,))
    return pl.pallas_call(
        functools.partial(last_kernel, fsdp, size, pieces, slack),
        out_shape=[
            jax.ShapeDtypeStruct(base.shape, F32), jax.ShapeDtypeStruct(small.shape, F32), jax.ShapeDtypeStruct(tapg.shape, F32),
            jax.ShapeDtypeStruct((model // fsdp, width), F32),
        ],
        in_specs=[vm] * 10, out_specs=[vm] * 4,
        scratch_shapes=[
            buf, pack, pack, pack, pltpu.VMEM(small.shape, F32), pltpu.VMEM((fsdp,) + small.shape, F32), pltpu.VMEM((size,) + small.shape, F32),
            pltpu.VMEM((fsdp,) + tapg.shape, F32), buf, buf, buf, buf,
            dma, dma, dma, dma, plane, plane, line, line, plane, plane, plane, plane, plane, plane,
        ],
        compiler_params=pltpu.CompilerParams(collective_id=collective_id, has_side_effects=True),
        cost_estimate=cost(55),
        name="last_sums",
    )(gproj, w_rows, normed_t, tokens, gain, gbranch_t, gated, base, small, tapg)


def norm_scale(values):
    return lax.rsqrt(jnp.mean(values * values, axis=-1, keepdims=True) + epsilon)


def norm_back(grad_normed, values, scale, gain):
    unit = values * scale
    gain_grad = jnp.sum(grad_normed * unit, axis=0)
    pulled = grad_normed * gain
    input_part = scale * (pulled - unit * jnp.mean(pulled * unit, axis=-1, keepdims=True))
    return (input_part, gain_grad)


def body(
    tokens, lengths, gain_mix, w_query, w_key, w_value, w_outgate, w_beta, w_decay,
    conv_query, conv_key, conv_value, decay_log, decay_bias, gain_head, w_out, gain_ff,
    w_gate, w_up, w_down, cotangent,
):
    fsdp, tp = lax.axis_size("fsdp"), lax.axis_size("tp")
    my_fsdp, my_tp = lax.axis_index("fsdp"), lax.axis_index("tp")
    shard_rows, d_model = tokens.shape
    w_rows = w_query.shape[0]
    heads = w_beta.shape[1]
    kw, vw = w_query.shape[1], w_value.shape[1]
    dk, dv = kw // heads, vw // heads
    conv_w = 2 * kw + vw
    main_w = conv_w + vw
    proj_w = main_w + 128
    ff = w_gate.shape[1]
    taps_n = conv_query.shape[0]

    taps_local = jnp.concatenate([conv_query, conv_key, conv_value], axis=1).reshape(1, -1)
    spare = 128 - 2 * heads
    tap_rows = -(-taps_local.shape[1] // spare)
    taps_pack = jnp.pad(taps_local, ((0, 0), (0, tap_rows * spare - taps_local.shape[1]))).reshape(tap_rows, spare)
    taps_pack = jnp.pad(taps_pack, ((0, w_rows - tap_rows), (0, 0)))
    extras = jnp.concatenate([w_beta, w_decay, taps_pack], axis=1)
    mix_pack = jnp.concatenate([jnp.transpose(a) for a in (w_query, w_key, w_value, w_outgate, extras)] + [w_out], axis=0)
    mix_pack, tokens = lax.optimization_barrier((mix_pack, tokens))
    mix_full = lax.all_gather(mix_pack, "fsdp", axis=1, tiled=True)
    n_mix, n_head = gain_mix.shape[0], gain_head.shape[0]
    gains_local = jnp.concatenate([gain_mix, gain_head, gain_ff]).astype(F32)
    gains_tile = jnp.pad(gains_local[None, :], ((0, 7), (0, 128 - gains_local.shape[0])))
    group_tokens, gains = line_gather(tokens, gains_tile, fsdp, tp, 2, 4)
    gains = jnp.transpose(gains[:, :, 0, :], (1, 0, 2)).reshape(tp * fsdp, 128)
    mix_gain = gains[:, :n_mix].reshape(-1)
    head_gain = gains[:, n_mix : n_mix + n_head].reshape(-1)
    ff_gain = gains[:, n_mix + n_head : 2 * n_mix + n_head].reshape(-1)
    live = my_tp * shard_rows + jnp.arange(shard_rows, dtype=jnp.int32) < lengths[0]
    grad_out = jnp.where(live[:, None], cotangent, jnp.zeros_like(cotangent))
    grad_out, group_tokens, mix_full = lax.optimization_barrier((grad_out, group_tokens, mix_full))
    group_grad_ff = lax.all_gather(grad_out, "tp", axis=0, tiled=True)
    wide = -(-ff // 128) * 128
    pad_wide = lambda a: jnp.pad(a, ((0, wide - ff), (0, 0)))
    ff_pack = jnp.concatenate([pad_wide(jnp.transpose(w_gate)), pad_wide(jnp.transpose(w_up)), pad_wide(w_down)], axis=0)

    taps_all = mix_full[main_w + 2 * heads : proj_w].reshape(spare, fsdp, w_rows)[:, :, :tap_rows]
    taps_all = jnp.transpose(taps_all, (1, 2, 0)).reshape(fsdp, -1)
    cq, cv = conv_query.shape[1], conv_value.shape[1]
    taps_all = taps_all[:, : taps_n * (2 * cq + cv)].reshape(fsdp, taps_n, 2 * cq + cv)
    taps_all = jnp.transpose(taps_all, (1, 0, 2))
    taps = jnp.concatenate(
        [taps_all[:, :, :cq].reshape(taps_n, -1), taps_all[:, :, cq : 2 * cq].reshape(taps_n, -1), taps_all[:, :, 2 * cq :].reshape(taps_n, -1)],
        axis=1,
    ).astype(F32)
    taps = jnp.pad(taps, ((0, 8 - taps_n), (0, 0)))
    log_f, bias_f = decay_log.astype(F32), decay_bias.astype(F32)
    pad_lanes = lambda v: jnp.pad(v, (heads, 128 - 2 * heads))[None, :]
    misc = jnp.pad(jnp.concatenate([pad_lanes(-jnp.exp(log_f)), pad_lanes(bias_f)], axis=0), ((0, 6), (0, 0)))
    gain_row = jnp.tile(head_gain, heads)[None, :]

    group_float = group_tokens.astype(F32)
    mix_scale = norm_scale(group_float)
    normed = (group_float * mix_scale * mix_gain).astype(BF16)
    ff_pack, normed = lax.optimization_barrier((ff_pack, normed))
    proj = lax.dot_general(normed, mix_full[:proj_w], NT, preferred_element_type=F32)
    gated, mixed, u, inverse, start, branch = mixer_fwd(
        proj, taps, misc, gain_row, mix_full, heads, dk, dv, tp, 2, 3)
    branch, group_grad_ff = lax.optimization_barrier((branch, group_grad_ff))
    ff_full = lax.all_gather(ff_pack, "fsdp", axis=1, tiled=True)
    group_state = group_float + branch
    own_rows = lambda full: lax.dynamic_slice_in_dim(full, my_tp * shard_rows, shard_rows, axis=0)
    hidden_state = own_rows(group_state)

    ff_normed, inner, grad_acts, ff_part, ff_gain_grad, sent_sum = feed_forward(
        group_tokens, branch, group_grad_ff, ff_gain[None, :], ff_full, wide, tp, 2, 5)
    ff_gain_grad = ff_gain_grad[0]
    ff_weight_grad = lax.dot_general(ff_normed, grad_acts, TN, preferred_element_type=F32)
    down_grad = lax.dot_general(group_grad_ff, inner, TN, preferred_element_type=F32)
    ff_grads = jnp.concatenate([ff_weight_grad.astype(BF16), down_grad.astype(BF16)], axis=1)
    sent_sum, ff_grads = lax.optimization_barrier((sent_sum, ff_grads))
    ff_sums = lax.psum_scatter(ff_grads, "fsdp", scatter_dimension=0, tiled=True).astype(F32)
    ff_branch = lax.psum_scatter(ff_part, "tp", scatter_dimension=0, tiled=True)
    group_grad_hidden = group_grad_ff.astype(F32) + sent_sum
    group_grad_branch = group_grad_hidden.astype(BF16)
    grad_hidden = own_rows(group_grad_hidden)

    grad_gated = lax.dot_general(group_grad_branch, mix_full[proj_w:], NT, preferred_element_type=F32)
    grad_projected, tap_grads, small, head_gain_grad = mixer_bwd(
        grad_gated, proj, taps, misc, gain_row, mixed, u, inverse, start, heads, dk, dv
    )
    head_part = jnp.sum(head_gain_grad[0].reshape(heads, dv), axis=0)
    decays = jnp.pad(jnp.concatenate([small[0, : 2 * heads], small[1, : 2 * heads]]), (0, 128 - 4 * heads))
    decays = jnp.where(jnp.arange(tp)[:, None] == my_tp, decays[None, :], 0.0).reshape(-1)
    others = jnp.pad(jnp.concatenate([head_part, decays]), (0, d_model - dv - tp * 128))
    small_rows = jnp.pad(jnp.stack([ff_gain_grad, others]), ((1, 5), (0, 0)))
    layer_out = jnp.where(live[:, None], hidden_state + ff_branch.astype(F32), 0.0).astype(BF16)
    input_grad, small_sums, tap_sums, mix_sums = last_sums(
        grad_projected, mix_full, jnp.transpose(normed), group_tokens, mix_gain[None, :], jnp.transpose(group_grad_branch), gated,
        grad_hidden, small_rows, tap_grads, fsdp, tp, 8, 2, 8)
    place = my_tp * fsdp + my_fsdp
    at = lambda row, start, n: lax.dynamic_slice(small_sums, (row, start), (1, n))[0]
    gain_mix_grad = at(0, place * n_mix, n_mix)
    gain_ff_grad = at(1, place * n_mix, n_mix)
    gain_head_grad = at(2, place * n_head, n_head)
    decay_sums = at(2, dv + my_tp * 128, 128)
    tap_at = lambda start, n: lax.dynamic_slice(tap_sums, (0, start + my_fsdp * n), (taps_n, n))
    return (
        layer_out,
        input_grad,
        gain_mix_grad,
        mix_sums[:, :kw],
        mix_sums[:, kw : 2 * kw],
        mix_sums[:, 2 * kw : conv_w],
        mix_sums[:, conv_w:main_w],
        mix_sums[:, main_w : main_w + heads],
        mix_sums[:, main_w + heads : main_w + 2 * heads],
        tap_at(0, cq),
        tap_at(kw, cq),
        tap_at(2 * kw, cv),
        decay_sums[heads : 2 * heads],
        decay_sums[3 * heads : 4 * heads],
        gain_head_grad,
        jnp.transpose(mix_sums[:, proj_w:]),
        gain_ff_grad,
        ff_sums[:, :ff],
        ff_sums[:, wide : wide + ff],
        jnp.transpose(ff_sums[:, 2 * wide : 2 * wide + ff]),
    )


def solution(mesh):
    placed = (
        P(("fsdp", "tp"), None),
        P("fsdp"),
        P(("tp", "fsdp")),
        P("fsdp", "tp"),
        P("fsdp", "tp"),
        P("fsdp", "tp"),
        P("fsdp", "tp"),
        P("fsdp", "tp"),
        P("fsdp", "tp"),
        P(None, ("tp", "fsdp")),
        P(None, ("tp", "fsdp")),
        P(None, ("tp", "fsdp")),
        P("tp"),
        P("tp"),
        P(("tp", "fsdp")),
        P("tp", "fsdp"),
        P(("tp", "fsdp")),
        P("fsdp", "tp"),
        P("fsdp", "tp"),
        P("tp", "fsdp"),
        P(("fsdp", "tp"), None),
    )
    return jax.shard_map(
        body,
        mesh=mesh,
        in_specs=placed,
        out_specs=(
            P(("fsdp", "tp"), None),
            P(("fsdp", "tp"), None),
            P(("tp", "fsdp")),
            P("fsdp", "tp"),
            P("fsdp", "tp"),
            P("fsdp", "tp"),
            P("fsdp", "tp"),
            P("fsdp", "tp"),
            P("fsdp", "tp"),
            P(None, ("tp", "fsdp")),
            P(None, ("tp", "fsdp")),
            P(None, ("tp", "fsdp")),
            P("tp"),
            P("tp"),
            P(("tp", "fsdp")),
            P("tp", "fsdp"),
            P(("tp", "fsdp")),
            P("fsdp", "tp"),
            P("fsdp", "tp"),
            P("tp", "fsdp"),
        ),
        check_vma=False,
    )
```

time: 1770 us -> 385 us (0.22); the launches traced: 1750 us -> 384 us
  waiting for transfers between devices: 662 us -> 2.58 us
  matrix products: 404 us -> 21.6 us
  local copies, waits for them, and re-layouts: 376 us -> 42 us
  Pallas kernels: 0 us -> 281 us
  other arithmetic: 151 us -> 21.9 us
  blocking collectives: 127 us -> 0 us
    reduce_scatter x12 -> x2, waiting for transfers between devices: 423 us -> 0.01 us  [the longest x1 0.01 us: body(): ff_branch = lax.psum_scatter(ff_part, 'tp', scatter_dimension=0, tiled=True)]
    dot_general x262 -> x4, matrix products: 404 us -> 21.6 us  [the longest x1 9.55 us: body(): lax.dot_general(normed, mix_full[:proj_w], NT, preferred_element_type=F32)]
    pallas_call x0 -> x5, Pallas kernels: none -> 281 us  [the longest x1 81.9 us: mixer_fwd(): pl.pallas_call(functools.partial(fwd_kernel, size, lag, heads, dk, dv), g...]
    all_gather x10 -> x3, waiting for transfers between devices: 170 us -> 2.5 us  [the longest x1 2.47 us: body(): ff_full = lax.all_gather(ff_pack, 'fsdp', axis=1, tiled=True)]
    squeeze x112 -> x3, local copies, waits for them, and re-layouts: 150 us -> 3.35 us  [the longest x2 2.59 us: body(): lax.dynamic_slice(small_sums, (row, start), (1, n))[0]]
    all_gather x9 -> x0, blocking collectives: 80.4 us -> none  [the longest x1 10.7 us: body(): lax.all_gather(w_key, 'fsdp', axis=0, tiled=True)]
    unnamed x32 -> x5, waiting for transfers between devices: 69 us -> 0.08 us
    unnamed x4 -> x0, blocking collectives: 46.3 us -> none
  transfers between devices with their start and end apart: 27 -> 5, of which waited for: 18 -> 1; matrix products, arithmetic and copies ran while one was open for 52% -> 18% of each run, Pallas kernels for 0% -> 56%
where the time goes in v1:
time: 385 us; the launch traced here: 384 us
  Pallas kernels  281 us (73%)
  local copies, waits for them, and re-layouts  42 us (11%)
  other arithmetic  21.9 us (6%)
  matrix products  21.6 us (6%)
  between operations  14.8 us (4%)
    pallas_call x1, Pallas kernels, mixer_fwd(): pl.pallas_call(functools.partial(fwd_kernel, size, lag, heads, dk, dv), g...  81.9 us
    pallas_call x1, Pallas kernels, last_sums(): pl.pallas_call(functools.partial(last_kernel, fsdp, size, pieces, slack),...  67.7 us
    pallas_call x1, Pallas kernels, feed_forward(): pl.pallas_call(functools.partial(ff_kernel, size, lag, wide), grid=(chunk...  65.1 us
    pallas_call x1, Pallas kernels, line_gather(): pl.pallas_call(functools.partial(line_gather_kernel, fsdp, size, pieces),...  39.6 us
    pallas_call x1, Pallas kernels, mixer_bwd(): pl.pallas_call(functools.partial(bwd_kernel, heads, dk, dv), grid=(chunks...  26.9 us
    unnamed x52, local copies, waits for them, and re-layouts  13.8 us
    dot_general x1, matrix products, body(): lax.dot_general(normed, mix_full[:proj_w], NT, preferred_element_type=F32)  9.55 us
  transfers between devices with their start and end apart: 5, of which 1 were waited for; matrix products, arithmetic and copies ran while one was open for 18% of the time, Pallas kernels for 56%

profile of v1, /device:TPU:12, one launch (start us, length us, event | category | flops | bytes accessed | tf_op | source)
XLA Modules:
  0.0 384.4 jit_solution(6242119638321591380)
XLA Ops:
  7.3 1.0 copy.54
  8.3 1.0 copy.55
  9.3 1.0 copy.56
  10.3 1.1 copy.57
  11.4 0.8 maximum_bitcast_fusion
  12.2 0.1 reshape.138
  12.3 0.1 copy.58
  12.5 0.7 fusion.17
  13.2 0.9 constant_dynamic-update-slice_fusion
  14.2 0.8 copy-done.6
  15.7 0.7 fusion.34.tile_ref
  16.4 39.6 %line_gather.1 = (bf16[1024,1024]{1,0:T(8,128)(2,1)}, f32[8,4,8,128]{3,2,1,0:T(8,128)}) custom-call(bf16[256,1024]{1,0:T(8,128)(2,1)} %x_ref, f32[8,128]{1,0:T(8,128)} %fusion.34.tile_ref), custom_call_target="tpu_custom_call" | custom-call | bytes 120000000 | tf_op jit(solution)/shard_map/line_gather/pallas_call | solution.py:668
  56.1 0.9 broadcast_select_fusion
  57.0 0.9 slice.90
  58.1 1.8 fusion.13
  59.9 0.5 multiply_reduce_fusion
  60.4 1.9 multiply_convert_fusion
  62.5 0.6 copy.73
  63.1 0.7 broadcast_in_dim_reshape.7.gain_ref
  63.9 0.6 select_maximum_fusion.2.misc_ref
  64.6 1.0 slice.93
  65.6 0.2 copy.71
  65.8 0.1 reshape.141
  66.3 0.6 fusion.24.taps_ref
  66.9 9.5 %fusion.proj_ref.before_ref = f32[1024,1664]{1,0:T(8,128)} fusion(bf16[1024,1024]{1,0:T(8,128)(2,1)} %multiply_convert_fusion, bf16[2176,1024]{1,0:T(8,128)(2,1)} %all-gather.4.cloned.1.call-done.out_w_ref.w_ref), kind=kOutput, calls=%fused_computation.5 | convolution fusion | flops 3489660928 | bytes 12320768 | tf_op jit(solution)/shard_map/dot_general | solution.py:1066
  76.5 81.9 %mixer_fwd.1 = (bf16[1024,512]{1,0:T(8,128)(2,1)}, f32[1024,512]{1,0:T(8,128)}, bf16[1024,512]{1,0:T(8,128)(2,1)}, bf16[1024,256]{1,0:T(8,128)(2,1)}, bf16[8,128...) custom-call(f32[1024,1664]{1,0:T(8,128)} %fusion.proj_ref.before_ref, f32[8,1024]{1,0:T(8,128)} %fusion.24.taps_ref, ...), custom_call_target="tpu_custom_call" | custom-call | bytes 195000000 | tf_op jit(solution)/shard_map/mixer_fwd/pallas_call | solution.py:292
  158.4 2.5 all-gather.8.cloned.1.call-done.w_ref
  160.9 65.1 %feed_forward.1 = (bf16[1024,1024]{1,0:T(8,128)(2,1)}, bf16[1024,768]{1,0:T(8,128)(2,1)}, bf16[1024,1536]{1,0:T(8,128)(2,1)}, bf16[1024,1024]{1,0:T(8,128)(2,1)}...) custom-call(bf16[1024,1024]{1,0:T(8,128)(2,1)} %get-tuple-element.56.tokens_ref, f32[1024,1024]{1,0:T(8,128)} %get-tuple-element.62.branch_ref, ...), custom_call_target="tpu_custom_call" | custom-call | bytes 195000000 | tf_op jit(solution)/shard_map/feed_forward/pallas_call | solution.py:524
  226.2 1.5 copy-done.3
  227.7 3.4 convolution_convert_fusion.1
  231.1 4.0 %convolution_convert_fusion = bf16[1024,1536]{1,0:T(8,128)(2,1)S(1)} fusion(bf16[1024,1024]{1,0:T(8,128)(2,1)S(1)} %copy-done.14, bf16[1024,1536]{1,0:T(8,128)(2,1)S(1)} %copy-done.13), kind=kOutput, calls=%fused_computation.4 | convolution fusion | flops 3222798336 | bytes 8388608 | tf_op jit(solution)/shard_map/dot_general | solution.py:1078
  235.1 2.4 pad_maximum_fusion
  237.6 0.7 broadcast_in_dim_reshape.8.gain_ref
  238.3 0.9 copy-done.1
  239.2 2.5 convert_element_type.63
  241.6 4.0 %copy.62.normed_ref = bf16[1024,1024]{1,0:T(8,128)(2,1)} copy(bf16[1024,1024]{0,1:T(8,128)(2,1)} %bitcast.76) | data formatting | bytes 4194304 | tf_op jit(solution)/shard_map/transpose | solution.py:1099
  245.6 3.8 convert_bitcast_fusion
  249.4 4.6 %fusion.9.grad_ref = f32[1024,512]{1,0:T(8,128)} fusion(bf16[2176,1024]{1,0:T(8,128)(2,1)} %all-gather.4.cloned.1.call-done.out_w_ref.w_ref, f32[1024,1024]{1,0:T(8,128)S(1)} %get-tuple-element.127), kind=kOutput, calls=%fused_computation.20 | convolution fusion | flops 1074790400 | bytes 7340032 | tf_op jit(solution)/shard_map/dot_general | solution.py:1088
  254.1 26.9 %mixer_bwd.1 = (bf16[1024,1664]{1,0:T(8,128)(2,1)}, f32[8,1024]{1,0:T(8,128)}, f32[8,128]{1,0:T(8,128)}, f32[8,512]{1,0:T(8,128)}) custom-call(f32[1024,512]{1,0:T(8,128)} %fusion.9.grad_ref, f32[1024,1664]{1,0:T(8,128)} %fusion.proj_ref.before_ref, f32[1024,1664]{1,0:T(8,128)} %fusion.proj_ref.before_ref, f32[8,1024]{1,0:T(8,128)} %fusion.24.taps_ref, ...), custom_call_target="tpu_custom_call" | custom-call | bytes 81000000 | tf_op jit(solution)/shard_map/mixer_bwd/pallas_call | solution.py:449
  281.0 0.7 slice_reduce_fusion
  281.7 0.8 slice.102
  282.5 2.7 copy.63.gbranch_ref
  285.2 0.8 slice_bitcast_fusion.7
  286.1 0.6 select_maximum_fusion.small_ref
  286.7 2.4 constant_dynamic-slice_fusion.4.base_ref
  289.2 67.7 %last_sums.1 = (f32[256,1024]{1,0:T(8,128)}, f32[8,1024]{1,0:T(8,128)}, f32[8,1024]{1,0:T(8,128)}, f32[128,2176]{1,0:T(8,128)}) custom-call(bf16[1024,1664]{1,0:T(8,128)(2,1)} %get-tuple-element.75.gproj_ref, bf16[2176,1024]{1,0:T(8,128)(2,1)} %all-gather.4.cloned.1.call-done.out_w_ref.w_ref, bf16[1024,1024]{1,0:T(8,128)(2,1)} %copy.62.normed_ref, ...), custom_call_target="tpu_custom_call" | custom-call | bytes 165000000 | tf_op jit(solution)/shard_map/last_sums/pallas_call | solution.py:974
  356.8 2.0 slice_bitcast_fusion.1
  358.8 0.8 copy.66
  359.6 1.0 fusion.38
  360.6 0.6 copy.64
  361.3 0.6 copy.65
  361.9 1.3 fusion.35
  363.1 0.7 constant_dynamic-slice_fusion.6
  363.9 1.3 dynamic-slice_bitcast_fusion
  365.2 1.3 constant_dynamic-slice_fusion
  366.6 1.3 constant_dynamic-slice_fusion.1
  367.9 0.6 slice_bitcast_fusion.4
  368.5 1.7 fusion.39
  370.2 2.6 fusion.8
  372.8 1.2 convert_element_type.72
  374.1 0.9 copy.69
  375.0 0.9 copy.67
  375.9 0.9 copy.68
  376.9 1.0 copy.85
  (77 shorter events, 1.7 us)
Async XLA Ops:
  7.2 8.5 %copy-start.12 = (bf16[32]{0:T(256)(128)(2,1)S(1)}, bf16[32]{0:T(256)(128)(2,1)}, u32[]{:S(2)}) copy-start(bf16[32]{0:T(256)(128)(2,1)} %param.23) | copy-start | bytes 196
  7.2 8.5 %copy-start.11 = (bf16[8]{0:T(256)(128)(2,1)S(1)}, bf16[8]{0:T(256)(128)(2,1)}, u32[]{:S(2)}) copy-start(bf16[8]{0:T(256)(128)(2,1)} %param.35) | copy-start | bytes 52
  7.2 8.5 %copy-start.10 = (bf16[32]{0:T(256)(128)(2,1)S(1)}, bf16[32]{0:T(256)(128)(2,1)}, u32[]{:S(2)}) copy-start(bf16[32]{0:T(256)(128)(2,1)} %param.37) | copy-start | bytes 196
  7.2 48.8 %copy-start.7 = (bf16[256,1024]{1,0:T(8,128)(2,1)S(1)}, bf16[256,1024]{1,0:T(8,128)(2,1)}, u32[]{:S(2)}) copy-start(bf16[256,1024]{1,0:T(8,128)(2,1)} %param.41) | copy-start | bytes 1572868
  7.2 49.7 %all-gather.4.cloned.1.call-start = ((), (), s32[]{:S(2)}) async-start(), calls=%async_computation.2 | async-start | bytes 5013504 | tf_op jit(solution)/shard_map/all_gather | solution.py:1030
  10.3 47.8 %copy-start.8 = (bf16[704,128]{1,0:T(8,128)(2,1)S(1)}, bf16[704,128]{1,0:T(8,128)(2,1)}, u32[]{:S(2)}) copy-start(bf16[704,128]{1,0:T(8,128)(2,1)} %param.40) | copy-start | bytes 540676
  10.3 47.8 %copy-start.9 = (bf16[128,704]{0,1:T(8,128)(2,1)S(1)}, bf16[128,704]{0,1:T(8,128)(2,1)}, u32[]{:S(2)}) copy-start(bf16[128,704]{0,1:T(8,128)(2,1)} %param.39) | copy-start | bytes 540676
  14.2 0.8 copy-start.6
  15.0 143.5 %all-gather.6.cloned.1.call-start = ((), (), s32[]{:S(2)}) async-start(), calls=%async_computation.3 | async-start | bytes 2621440 | tf_op jit(solution)/shard_map/all_gather | solution.py:1042
  56.0 3.9 %copy-start = (bf16[1024,1024]{1,0:T(8,128)(2,1)S(1)}, bf16[1024,1024]{1,0:T(8,128)(2,1)}, u32[]{:S(2)}) copy-start(bf16[1024,1024]{1,0:T(8,128)(2,1)} %get-tuple-element.56.tokens_ref) | copy-start | bytes 6291460
  57.0 103.9 %all-gather.8.cloned.1.call-start = ((), (), s32[]{:S(2)}) async-start(), calls=%async_computation.4 | async-start | bytes 5308416 | tf_op jit(solution)/shard_map/all_gather | solution.py:1070
  60.4 3.4 copy-start.15
  60.4 3.5 copy-start.16
  62.3 307.9 %reduce-scatter.3.cloned.1.call-start = ((), (), s32[]{:S(2)}) async-start(), calls=%async_computation.5 | async-start | bytes 2621440 | tf_op jit(solution)/shard_map/reduce_scatter | solution.py:1083
  226.1 1.6 copy-start.3
  226.1 146.7 %reduce-scatter.5.cloned.1.call-start = ((), (), s32[]{:S(2)}) async-start(), calls=%async_computation.6 | async-start | bytes 5308416 | tf_op jit(solution)/shard_map/reduce_scatter | solution.py:1082
  227.7 3.4 copy-start.13
  227.7 3.4 copy-start.14
  237.6 1.6 copy-start.1
  249.4 4.6 %copy-start.2 = (f32[1024,1024]{1,0:T(8,128)}, f32[1024,1024]{1,0:T(8,128)S(1)}, u32[]{:S(2)}) copy-start(f32[1024,1024]{1,0:T(8,128)S(1)} %get-tuple-element.127) | copy-start | bytes 12582916
  372.8 2.2 copy-start.4
  374.1 2.8 copy-start.5
Sparse Core Ops, SparseCore 0:
  15.1 39.2 all-gather.3
  57.1 59.9 all-gather.5
  119.6 41.2 all-gather.7
  226.2 44.7 reduce-scatter.2
  274.3 60.0 reduce-scatter.4

commit v2 on v1

--- a/solution.py
+++ b/solution.py
@@ -211,6 +211,86 @@
                     self.left(self.to_left, p).wait_send()
 
 
+class StreamGather:
+    def __init__(self, size, pieces, x_ref, out_ref, own_sem, sl, sr, rl, rr):
+        self.size, self.pieces = size, pieces
+        self.me = lax.axis_index("tp")
+        self.x, self.out, self.own_sem = x_ref, out_ref, own_sem
+        self.sl, self.sr, self.rl, self.rr = sl, sr, rl, rr
+        self.shard = x_ref.shape[0]
+        self.rows = self.shard // pieces
+
+    def region(self, s, k):
+        return self.out.at[pl.ds(pl.multiple_of(s * self.shard + k * self.rows, self.rows), self.rows), :]
+
+    def to_right(self, src, s, k):
+        return pltpu.make_async_remote_copy(
+            src_ref=src, dst_ref=self.region(s, k), send_sem=self.sr.at[s * self.pieces + k], recv_sem=self.rl.at[s * self.pieces + k],
+            device_id={"tp": jnp.minimum(self.me + 1, self.size - 1)}, device_id_type=MESH)
+
+    def to_left(self, src, s, k):
+        return pltpu.make_async_remote_copy(
+            src_ref=src, dst_ref=self.region(s, k), send_sem=self.sl.at[s * self.pieces + k], recv_sem=self.rr.at[s * self.pieces + k],
+            device_id={"tp": jnp.maximum(self.me - 1, 0)}, device_id_type=MESH)
+
+    def own(self):
+        here = pl.ds(pl.multiple_of(self.me * self.shard, self.shard), self.shard)
+        return pltpu.make_async_copy(self.x, self.out.at[here, :], self.own_sem)
+
+    def start(self):
+        self.own().start()
+        for k in range(self.pieces):
+            src = self.x.at[pl.ds(k * self.rows, self.rows), :]
+
+            @pl.when(self.me < self.size - 1)
+            def _():
+                self.to_right(src, self.me, k).start()
+
+            @pl.when(self.me > 0)
+            def _():
+                self.to_left(src, self.me, k).start()
+
+    def tick(self, t):
+        d = t // self.pieces + 1
+        k = t % self.pieces
+        s_left, s_right = self.me - d, self.me + d
+
+        @pl.when((t >= 0) & (d < self.size) & (s_left >= 0))
+        def _():
+            self.to_right(self.region(s_left, k), s_left, k).wait_recv()
+
+            @pl.when(self.me < self.size - 1)
+            def _():
+                self.to_right(self.region(s_left, k), s_left, k).start()
+
+        @pl.when((t >= 0) & (d < self.size) & (s_right < self.size))
+        def _():
+            self.to_left(self.region(s_right, k), s_right, k).wait_recv()
+
+            @pl.when(self.me > 0)
+            def _():
+                self.to_left(self.region(s_right, k), s_right, k).start()
+
+    def finish(self, steps):
+        @pl.loop(steps - 1, max((self.size - 1) * self.pieces, steps - 1))
+        def _(t):
+            self.tick(t)
+
+        self.own().wait()
+
+        @pl.loop(0, self.size * self.pieces)
+        def _(t):
+            s, k = t // self.pieces, t % self.pieces
+
+            @pl.when((self.me < self.size - 1) & (s <= self.me))
+            def _():
+                self.to_right(self.region(s, k), s, k).wait_send()
+
+            @pl.when((self.me > 0) & (s >= self.me))
+            def _():
+                self.to_left(self.region(s, k), s, k).wait_send()
+
+
 def stream_scratch(rows, width):
     buf = pltpu.VMEM((rows, width), BF16)
     dma = pltpu.SemaphoreType.DMA((rows // PIECE,))
@@ -218,21 +298,27 @@
 
 
 def fwd_kernel(
-    size, lag, heads, dk, dv, proj_ref, taps_ref, misc_ref, gain_ref, out_w_ref, gated_ref, mixed_ref, u_ref, inv_ref, start_ref, sum_ref,
-    ext_ref, state_ref, x_ref, *line_refs
+    size, lag, heads, dk, dv, tokens_ref, norm_gain_ref, taps_ref, misc_ref, gain_ref, out_w_ref, shard_ref,
+    normed_ref, proj_ref, gated_ref, mixed_ref, u_ref, inv_ref, start_ref, sum_ref, whole_ref, landed, own_sem, gsl, gsr, grl, grr, ext_ref, state_ref, x_ref, *line_refs
 ):
     rows = CHUNK
     step = pl.program_id(0)
     line = StreamSum(size, lag, pl.num_programs(0), x_ref, sum_ref, *line_refs)
+    gather = StreamGather(size, 2, shard_ref, landed, own_sem, gsl, gsr, grl, grr)
     kw, vw = heads * dk, heads * dv
     conv_w = 2 * kw + vw
 
     @pl.when(step == 0)
     def _():
         line_barrier(line.me, size)
+        gather.start()
         ext_ref[0:8, :] = jnp.zeros((8, conv_w), F32)
         state_ref[...] = jnp.zeros_like(state_ref)
 
+    values = tokens_ref[...].astype(F32)
+    normed = (values * lax.rsqrt(jnp.mean(values * values, axis=-1, keepdims=True) + epsilon) * norm_gain_ref[...]).astype(BF16)
+    normed_ref[...] = normed
+    proj_ref[...] = mm(normed, out_w_ref[0 : conv_w + vw + 128, :], NT)
     ext_ref[pl.ds(8, rows), :] = proj_ref[:, 0:conv_w]
     conv = conv_rows(ext_ref, taps_ref, rows)
     ext_ref[0:8, :] = ext_ref[pl.ds(rows, 8), :]
@@ -275,45 +361,60 @@
         branch = part if h == 0 else branch + part
         if h == 0:
             line.advance(2 * step)
+    gather.tick(step - 1)
     x_ref[pl.ds(pl.multiple_of(step * rows, rows), rows), :] = branch.astype(BF16)
     line.send_own(step)
     line.advance(2 * step + 1)
     line.finish(step)
 
-
-def mixer_fwd(proj, taps, misc, gain, out_w, heads, dk, dv, size, lag, collective_id):
-    total_rows, width = proj.shape
+    @pl.when(step == pl.num_programs(0) - 1)
+    def _():
+        gather.finish(total_steps(tokens_ref, sum_ref))
+        whole_ref[...] = landed[...]
+
+
+def total_steps(block_ref, whole_ref):
+    return whole_ref.shape[0] // block_ref.shape[0]
+
+
+def mixer_fwd(tokens, norm_gain, taps, misc, gain, out_w, shard, heads, dk, dv, size, lag, collective_id):
+    total_rows = tokens.shape[0]
     chunks = total_rows // CHUNK
     vw = heads * dv
     conv_w = 2 * heads * dk + vw
     model = out_w.shape[1]
+    width = conv_w + vw + 128
     blk = lambda w: pl.BlockSpec((CHUNK, w), lambda c: (c, 0))
     full = lambda a: pl.BlockSpec(a.shape, lambda c: (0, 0))
     return pl.pallas_call(
         functools.partial(fwd_kernel, size, lag, heads, dk, dv),
         grid=(chunks,),
-        in_specs=[blk(width), full(taps), full(misc), full(gain), full(out_w)],
+        in_specs=[blk(model), full(norm_gain), full(taps), full(misc), full(gain), full(out_w), full(shard)],
         out_specs=[
-            blk(vw), blk(vw), blk(vw), blk(heads * CHUNK), pl.BlockSpec((1, dk, vw), lambda c: (c, 0, 0)),
-            pl.BlockSpec((total_rows, model), lambda c: (0, 0)),
+            blk(model), blk(width), blk(vw), blk(vw), blk(vw), blk(heads * CHUNK), pl.BlockSpec((1, dk, vw), lambda c: (c, 0, 0)),
+            pl.BlockSpec((total_rows, model), lambda c: (0, 0)), pl.BlockSpec((total_rows, model), lambda c: (0, 0)),
         ],
         out_shape=[
+            jax.ShapeDtypeStruct((total_rows, model), BF16),
+            jax.ShapeDtypeStruct((total_rows, width), F32),
             jax.ShapeDtypeStruct((total_rows, vw), BF16),
             jax.ShapeDtypeStruct((total_rows, vw), F32),
             jax.ShapeDtypeStruct((total_rows, vw), BF16),
             jax.ShapeDtypeStruct((total_rows, heads * CHUNK), BF16),
             jax.ShapeDtypeStruct((chunks, dk, vw), BF16),
             jax.ShapeDtypeStruct((total_rows, model), F32),
+            jax.ShapeDtypeStruct((total_rows, model), shard.dtype),
         ],
-        scratch_shapes=[pltpu.VMEM((8 + CHUNK, conv_w), F32), pltpu.VMEM((dk, vw), F32)] + stream_scratch(total_rows, model),
+        scratch_shapes=[pltpu.VMEM((total_rows, model), BF16), pltpu.SemaphoreType.DMA] + [pltpu.SemaphoreType.DMA((size * 2,))] * 4
+        + [pltpu.VMEM((8 + CHUNK, conv_w), F32), pltpu.VMEM((dk, vw), F32)] + stream_scratch(total_rows, model),
         compiler_params=pltpu.CompilerParams(collective_id=collective_id, has_side_effects=True),
-        cost_estimate=cost(65),
+        cost_estimate=cost(88),
         name="mixer_fwd",
-    )(proj, taps, misc, gain, out_w)
-
-
-def bwd_kernel(heads, dk, dv, grad_ref, proj_ref, before_ref, taps_ref, misc_ref, gain_ref, mixed_ref, u_ref, inv_ref, start_ref,
-               gproj_ref, tapg_ref, small_ref, gaing_ref, ext_ref, back_ref, dstate_ref):
+    )(tokens, norm_gain, taps, misc, gain, out_w, shard)
+
+
+def bwd_kernel(heads, dk, dv, out_grad_ref, sent_ref, w_ref, proj_ref, before_ref, taps_ref, misc_ref, gain_ref, mixed_ref, u_ref, inv_ref,
+               start_ref, gbranch_ref, gproj_ref, tapg_ref, small_ref, gaing_ref, ext_ref, back_ref, dstate_ref):
     rows = CHUNK
     kw, vw = heads * dk, heads * dv
     conv_w = 2 * kw + vw
@@ -328,6 +429,9 @@
         small_ref[...] = jnp.zeros_like(small_ref)
         gaing_ref[...] = jnp.zeros_like(gaing_ref)
 
+    gbranch = (out_grad_ref[...].astype(F32) + sent_ref[...]).astype(BF16)
+    gbranch_ref[...] = gbranch
+    grad_gated = mm(gbranch, w_ref[conv_w + vw + 128 :, :], NT)
     ext_ref[0:8, :] = jnp.where(chunk > 0, before_ref[:, 0:conv_w], 0.0)
     ext_ref[pl.ds(8, rows), :] = proj_ref[:, 0:conv_w]
     conv = conv_rows(ext_ref, taps_ref, rows)
@@ -346,7 +450,7 @@
         gate = proj_ref[:, conv_w + h * dv : conv_w + (h + 1) * dv]
         gsig = sigmoid(gate)
         mixed = mixed_ref[:, cols]
-        grad = grad_ref[:, cols].astype(F32)
+        grad = grad_gated[:, cols]
         gain = gain_ref[:, cols]
         scale = lax.rsqrt(jnp.mean(mixed * mixed, axis=-1, keepdims=True) + epsilon)
         unit = mixed * scale
@@ -437,12 +541,13 @@
     back_ref[pl.ds(rows, 8), :] = back_ref[0:8, :]
 
 
-def mixer_bwd(grad, proj, taps, misc, gain, mixed, u, inverse, start, heads, dk, dv):
+def mixer_bwd(out_grad, sent, w_rows, proj, taps, misc, gain, mixed, u, inverse, start, heads, dk, dv):
     total_rows, width = proj.shape
     chunks = total_rows // CHUNK
     conv_w = 2 * heads * dk + heads * dv
     vw = heads * dv
     last = chunks - 1
+    model = out_grad.shape[1]
     blk = lambda w: pl.BlockSpec((CHUNK, w), lambda c: (last - c, 0))
     full = lambda a: pl.BlockSpec(a.shape, lambda c: (0, 0))
     per = CHUNK // 8
@@ -450,18 +555,19 @@
         functools.partial(bwd_kernel, heads, dk, dv),
         grid=(chunks,),
         in_specs=[
-            blk(vw), blk(width),
+            blk(model), blk(model), full(w_rows), blk(width),
             pl.BlockSpec((8, width), lambda c: (jnp.maximum((last - c) * per - 1, 0), 0)),
             full(taps), full(misc), full(gain), blk(vw), blk(vw), blk(heads * CHUNK),
             pl.BlockSpec((1, dk, vw), lambda c: (last - c, 0, 0)),
         ],
         out_specs=[
-            blk(width),
+            blk(model), blk(width),
             pl.BlockSpec((8, conv_w), lambda c: (0, 0)),
             pl.BlockSpec((8, 128), lambda c: (0, 0)),
             pl.BlockSpec((8, vw), lambda c: (0, 0)),
         ],
         out_shape=[
+            jax.ShapeDtypeStruct((total_rows, model), BF16),
             jax.ShapeDtypeStruct((total_rows, width), BF16),
             jax.ShapeDtypeStruct((8, conv_w), F32),
             jax.ShapeDtypeStruct((8, 128), F32),
@@ -474,7 +580,7 @@
         ],
         cost_estimate=cost(27),
         name="mixer_bwd",
-    )(grad, proj, proj, taps, misc, gain, mixed, u, inverse, start)
+    )(out_grad, sent, w_rows, proj, proj, taps, misc, gain, mixed, u, inverse, start)
 
 
 def ff_kernel(
@@ -740,6 +846,15 @@
                 if flip:
                     self.copy(stage + 1, i).start()
 
+    def advance_pair(self, pair):
+        i = self.place(pair)
+        g, total = self.total(0, i)
+        self.acc[self.rows(g), self.cols] = total.astype(BF16)
+
+        @pl.when(i % 2 != self.bit(self.order[1]))
+        def _():
+            self.copy(1, i // 2).start()
+
     def finish(self):
         @pl.loop(0, self.n // 2)
         def _(i):
@@ -866,35 +981,56 @@
     many = max(256 // block, 2)
     groups = fsdp // many
     ticks = count + (size - 2) * slack
-    per = max(ticks // (3 * groups), 1)
+    per = max(3 * ticks // (7 * groups), 1)
+    pairs = many // 2
+
+    def group_at(i):
+        mine, other = me_f // many, groups - 1 - i
+        total = 0
+        for b in halving_orders(groups)[0]:
+            total = total + ((mine // b + other // b) % 2) * b
+        return total
+
+    def advance_group(i):
+        @pl.loop(0, pairs)
+        def _(m):
+            for plane in planes:
+                plane.advance_pair(group_at(i) * pairs + m)
 
     @pl.loop(0, groups)
     def _(i):
-        here = pl.ds(pl.multiple_of(i * many * block, many * block), many * block)
-        grads[here, 0:proj_w] = mm(normed_ref[here, :], gproj_ref[...]).astype(BF16)
-        grads[here, proj_w:width] = mm(gbranch_ref[here, :], gated_ref[...]).astype(BF16)
-
-        @pl.loop(0, many // 2)
+        g = group_at(i)
+        here = pl.ds(pl.multiple_of(g * many * block, many * block), many * block)
+        grads[here, 0:proj_w] = mm(normed_ref[:, here], gproj_ref[...], TN).astype(BF16)
+        grads[here, proj_w:width] = mm(gbranch_ref[:, here], gated_ref[...], TN).astype(BF16)
+
+        @pl.loop(0, pairs)
         def _(m):
             for plane in planes:
-                plane.copy(0, plane.place(i * (many // 2) + m)).start()
+                plane.copy(0, plane.place(g * pairs + m)).start()
 
         @pl.loop(i * per, (i + 1) * per)
         def _(t):
             exchange(t)
 
+        @pl.when(i > 0)
+        def _():
+            advance_group(i - 1)
+
+    advance_group(groups - 1)
     stages = len(order_a)
     done = groups * per
     for stage in range(stages):
-        until = max(done, int(ticks * (0.4 + 0.45 * stage / max(stages - 1, 1))))
-
-        @pl.loop(done, until)
-        def _(t):
-            exchange(t)
-
-        done = until
-        for plane in planes:
-            plane.advance(stage)
+        if stage > 0:
+            until = max(done, int(ticks * (0.68 + 0.24 * (stage - 1) / max(stages - 2, 1))))
+
+            @pl.loop(done, until)
+            def _(t):
+                exchange(t)
+
+            done = until
+            for plane in planes:
+                plane.advance(stage)
         if stage == 0:
             small_out[...] = small[...]
             tap_out[...] = tapg_ref[...]
@@ -963,7 +1099,7 @@
             left_copy(to_left, s, k).wait_send()
 
 
-def last_sums(gproj, w_rows, normed_t, tokens, gain, gbranch_t, gated, base, small, tapg, fsdp, size, pieces, slack, collective_id):
+def last_sums(gproj, w_rows, normed, tokens, gain, gbranch, gated, base, small, tapg, fsdp, size, pieces, slack, collective_id):
     vm = pl.BlockSpec(memory_space=pltpu.VMEM)
     total_rows, model = tokens.shape
     width = gproj.shape[1] + gated.shape[1]
@@ -986,7 +1122,7 @@
         compiler_params=pltpu.CompilerParams(collective_id=collective_id, has_side_effects=True),
         cost_estimate=cost(55),
         name="last_sums",
-    )(gproj, w_rows, normed_t, tokens, gain, gbranch_t, gated, base, small, tapg)
+    )(gproj, w_rows, normed, tokens, gain, gbranch, gated, base, small, tapg)
 
 
 def norm_scale(values):
@@ -1038,8 +1174,6 @@
     ff_gain = gains[:, n_mix + n_head : 2 * n_mix + n_head].reshape(-1)
     live = my_tp * shard_rows + jnp.arange(shard_rows, dtype=jnp.int32) < lengths[0]
     grad_out = jnp.where(live[:, None], cotangent, jnp.zeros_like(cotangent))
-    grad_out, group_tokens, mix_full = lax.optimization_barrier((grad_out, group_tokens, mix_full))
-    group_grad_ff = lax.all_gather(grad_out, "tp", axis=0, tiled=True)
     wide = -(-ff // 128) * 128
     pad_wide = lambda a: jnp.pad(a, ((0, wide - ff), (0, 0)))
     ff_pack = jnp.concatenate([pad_wide(jnp.transpose(w_gate)), pad_wide(jnp.transpose(w_up)), pad_wide(w_down)], axis=0)
@@ -1059,18 +1193,11 @@
     misc = jnp.pad(jnp.concatenate([pad_lanes(-jnp.exp(log_f)), pad_lanes(bias_f)], axis=0), ((0, 6), (0, 0)))
     gain_row = jnp.tile(head_gain, heads)[None, :]
 
-    group_float = group_tokens.astype(F32)
-    mix_scale = norm_scale(group_float)
-    normed = (group_float * mix_scale * mix_gain).astype(BF16)
-    ff_pack, normed = lax.optimization_barrier((ff_pack, normed))
-    proj = lax.dot_general(normed, mix_full[:proj_w], NT, preferred_element_type=F32)
-    gated, mixed, u, inverse, start, branch = mixer_fwd(
-        proj, taps, misc, gain_row, mix_full, heads, dk, dv, tp, 2, 3)
-    branch, group_grad_ff = lax.optimization_barrier((branch, group_grad_ff))
+    normed, proj, gated, mixed, u, inverse, start, branch, group_grad_ff = mixer_fwd(
+        group_tokens, mix_gain[None, :], taps, misc, gain_row, mix_full, grad_out, heads, dk, dv, tp, 2, 3)
     ff_full = lax.all_gather(ff_pack, "fsdp", axis=1, tiled=True)
-    group_state = group_float + branch
     own_rows = lambda full: lax.dynamic_slice_in_dim(full, my_tp * shard_rows, shard_rows, axis=0)
-    hidden_state = own_rows(group_state)
+    hidden_state = tokens.astype(F32) + own_rows(branch)
 
     ff_normed, inner, grad_acts, ff_part, ff_gain_grad, sent_sum = feed_forward(
         group_tokens, branch, group_grad_ff, ff_gain[None, :], ff_full, wide, tp, 2, 5)
@@ -1081,14 +1208,12 @@
     sent_sum, ff_grads = lax.optimization_barrier((sent_sum, ff_grads))
     ff_sums = lax.psum_scatter(ff_grads, "fsdp", scatter_dimension=0, tiled=True).astype(F32)
     ff_branch = lax.psum_scatter(ff_part, "tp", scatter_dimension=0, tiled=True)
-    group_grad_hidden = group_grad_ff.astype(F32) + sent_sum
-    group_grad_branch = group_grad_hidden.astype(BF16)
-    grad_hidden = own_rows(group_grad_hidden)
-
-    grad_gated = lax.dot_general(group_grad_branch, mix_full[proj_w:], NT, preferred_element_type=F32)
-    grad_projected, tap_grads, small, head_gain_grad = mixer_bwd(
-        grad_gated, proj, taps, misc, gain_row, mixed, u, inverse, start, heads, dk, dv
+    grad_hidden = grad_out.astype(F32) + own_rows(sent_sum)
+
+    group_grad_branch, grad_projected, tap_grads, small, head_gain_grad = mixer_bwd(
+        group_grad_ff, sent_sum, mix_full, proj, taps, misc, gain_row, mixed, u, inverse, start, heads, dk, dv
     )
+    ff_branch, grad_projected = lax.optimization_barrier((ff_branch, grad_projected))
     head_part = jnp.sum(head_gain_grad[0].reshape(heads, dv), axis=0)
     decays = jnp.pad(jnp.concatenate([small[0, : 2 * heads], small[1, : 2 * heads]]), (0, 128 - 4 * heads))
     decays = jnp.where(jnp.arange(tp)[:, None] == my_tp, decays[None, :], 0.0).reshape(-1)
@@ -1096,7 +1221,7 @@
     small_rows = jnp.pad(jnp.stack([ff_gain_grad, others]), ((1, 5), (0, 0)))
     layer_out = jnp.where(live[:, None], hidden_state + ff_branch.astype(F32), 0.0).astype(BF16)
     input_grad, small_sums, tap_sums, mix_sums = last_sums(
-        grad_projected, mix_full, jnp.transpose(normed), group_tokens, mix_gain[None, :], jnp.transpose(group_grad_branch), gated,
+        grad_projected, mix_full, normed, group_tokens, mix_gain[None, :], group_grad_branch, gated,
         grad_hidden, small_rows, tap_grads, fsdp, tp, 8, 2, 8)
     place = my_tp * fsdp + my_fsdp
     at = lambda row, start, n: lax.dynamic_slice(small_sums, (row, start), (1, n))[0]

time: 385 us -> 368 us (0.956)
  Pallas kernels: 281 us -> 299 us
  matrix products: 21.6 us -> 7.45 us
  local copies, waits for them, and re-layouts: 42 us -> 32 us
  other arithmetic: 21.9 us -> 13 us
    dot_general x2 -> x0, matrix products: 14.2 us -> none  [the longest x1 9.55 us: body(): lax.dot_general(normed, mix_full[:proj_w], NT, preferred_element_type=F32)]
    pallas_call x1, Pallas kernels: 81.9 us -> 91.3 us  [mixer_fwd(): pl.pallas_call(functools.partial(fwd_kernel, size, lag, heads, dk, dv), g...]
    convert_element_type x3 -> x0, other arithmetic: 6.95 us -> none  [the longest x1 2.64 us: body(): jnp.where(live[:, None], hidden_state + ff_branch.astype(F32), 0.0)]
    transpose x2 -> x0, local copies, waits for them, and re-layouts: 6.63 us -> none  [the longest x1 3.97 us: body(): jnp.transpose(normed)]
    pallas_call x1, Pallas kernels: 67.7 us -> 73.2 us  [last_sums(): pl.pallas_call(functools.partial(last_kernel, fsdp, size, pieces, slack),...]
    pallas_call x1, Pallas kernels: 26.9 us -> 30.9 us  [mixer_bwd(): pl.pallas_call(functools.partial(bwd_kernel, heads, dk, dv), grid=(chunks...]
    unnamed x52 -> x50, local copies, waits for them, and re-layouts: 13.8 us -> 12.9 us
  transfers between devices with their start and end apart: 5 -> 4, of which waited for: 1 -> 0; matrix products, arithmetic and copies ran while one was open for 18% -> 10% of each run, Pallas kernels for 56% -> 64%
where the time goes in v2:
time: 368 us; the launch traced here: 367 us
  Pallas kernels  299 us (81%)
  local copies, waits for them, and re-layouts  32 us (9%)
  between operations  14.8 us (4%)
  other arithmetic  13 us (4%)
  matrix products  7.45 us (2%)
    pallas_call x1, Pallas kernels, mixer_fwd(): pl.pallas_call(functools.partial(fwd_kernel, size, lag, heads, dk, dv), g...  91.3 us
    pallas_call x1, Pallas kernels, last_sums(): pl.pallas_call(functools.partial(last_kernel, fsdp, size, pieces, slack),...  73.2 us
    pallas_call x1, Pallas kernels, feed_forward(): pl.pallas_call(functools.partial(ff_kernel, size, lag, wide), grid=(chunk...  64 us
    pallas_call x1, Pallas kernels, line_gather(): pl.pallas_call(functools.partial(line_gather_kernel, fsdp, size, pieces),...  39.7 us
    pallas_call x1, Pallas kernels, mixer_bwd(): pl.pallas_call(functools.partial(bwd_kernel, heads, dk, dv), grid=(chunks...  30.9 us
    unnamed x50, local copies, waits for them, and re-layouts  12.9 us
  transfers between devices with their start and end apart: 4, of which 0 were waited for; matrix products, arithmetic and copies ran while one was open for 10% of the time, Pallas kernels for 64%

profile of v2, /device:TPU:12, one launch (start us, length us, event | category | flops | bytes accessed | tf_op | source)
XLA Modules:
  0.0 366.6 jit_solution(3210827381277741654)
XLA Ops:
  7.3 1.1 copy.52
  8.4 1.0 copy.53
  9.4 1.0 copy.54
  10.4 1.0 copy.55
  11.5 0.8 maximum_bitcast_fusion
  12.4 0.1 reshape.129
  12.4 0.1 copy.56
  12.7 0.7 fusion.9
  13.4 0.9 constant_dynamic-update-slice_fusion
  14.3 0.8 copy-done.5
  15.2 0.9 fusion.5
  16.8 0.7 fusion.26.tile_ref
  17.5 39.7 %line_gather.1 = (bf16[1024,1024]{1,0:T(8,128)(2,1)}, f32[8,4,8,128]{3,2,1,0:T(8,128)}) custom-call(bf16[256,1024]{1,0:T(8,128)(2,1)} %x_ref, f32[8,128]{1,0:T(8,128)} %fusion.26.tile_ref), custom_call_target="tpu_custom_call" | custom-call | bytes 120000000 | tf_op jit(solution)/shard_map/line_gather/pallas_call | solution.py:774
  57.2 0.9 slice.84
  58.1 0.1 slice.119
  58.3 0.7 broadcast_in_dim_reshape.7.norm_gain_ref.gain_ref
  58.9 0.1 tile.7
  59.0 0.6 copy.69
  59.6 0.7 broadcast_in_dim_reshape.8.gain_ref
  60.3 0.1 pad_bitcast_fusion
  60.4 0.1 bitcast_convert_fusion
  60.5 0.6 select_maximum_fusion.2.misc_ref
  61.1 0.9 broadcast_select_fusion.shard_ref
  62.0 1.0 slice.113
  63.0 0.2 copy.67
  63.2 0.1 reshape.132
  63.3 0.1 slice.118
  63.4 0.1 fusion.34
  63.5 0.1 reshape.134
  63.5 0.1 reshape.135
  63.6 0.1 reshape.136
  63.7 0.6 fusion.16.taps_ref
  64.3 91.3 %mixer_fwd.1 = (bf16[1024,1024]{1,0:T(8,128)(2,1)}, f32[1024,1664]{1,0:T(8,128)}, bf16[1024,512]{1,0:T(8,128)(2,1)}, f32[1024,512]{1,0:T(8,128)}, bf16[1024,512]...) custom-call(bf16[1024,1024]{1,0:T(8,128)(2,1)} %get-tuple-element.53, ...), custom_call_target="tpu_custom_call" | custom-call | bytes 264000000 | tf_op jit(solution)/shard_map/mixer_fwd/pallas_call | solution.py:389
  155.7 64.0 %feed_forward.1 = (bf16[1024,1024]{1,0:T(8,128)(2,1)}, bf16[1024,768]{1,0:T(8,128)(2,1)}, bf16[1024,1536]{1,0:T(8,128)(2,1)}, bf16[1024,1024]{1,0:T(8,128)(2,1)}...) custom-call(bf16[1024,1024]{1,0:T(8,128)(2,1)} %get-tuple-element.53.tokens_ref, f32[1024,1024]{1,0:T(8,128)} %get-tuple-element.56.branch_ref, ...), custom_call_target="tpu_custom_call" | custom-call | bytes 195000000 | tf_op jit(solution)/shard_map/feed_forward/pallas_call | solution.py:630
  219.8 1.5 copy-done
  221.3 3.4 convolution_convert_fusion.1
  224.8 4.0 %convolution_convert_fusion = bf16[1024,1536]{1,0:T(8,128)(2,1)S(1)} fusion(bf16[1024,1024]{1,0:T(8,128)(2,1)S(1)} %copy-done.13, bf16[1024,1536]{1,0:T(8,128)(2,1)S(1)} %copy-done.12), kind=kOutput, calls=%fused_computation.1 | convolution fusion | flops 3222798336 | bytes 8388608 | tf_op jit(solution)/shard_map/dot_general | solution.py:1205
  228.8 2.5 pad_maximum_fusion
  231.4 30.9 %mixer_bwd.1 = (bf16[1024,1024]{1,0:T(8,128)(2,1)}, bf16[1024,1664]{1,0:T(8,128)(2,1)}, f32[8,1024]{1,0:T(8,128)}, f32[8,128]{1,0:T(8,128)}, f32[8,512]{1,0:T(8,128)}) custom-call(bf16[1024,1024]{1,0:T(8,128)(2,1)} %get-tuple-element.57.grad_ref.out_grad_ref, f32[1024,1024]{1,0:T(8,128)} %get-tuple-element.63.sent_ref, ...), custom_call_target="tpu_custom_call" | custom-call | bytes 81000000 | tf_op jit(solution)/shard_map/mixer_bwd/pallas_call | solution.py:554
  262.2 0.7 slice_reduce_fusion
  263.0 0.8 slice.94
  263.8 0.8 slice_bitcast_fusion.7
  264.5 0.1 fusion.28
  264.6 0.1 select_bitcast_fusion
  264.7 0.6 select_maximum_fusion.small_ref
  265.3 3.1 dynamic-slice_add_fusion
  268.5 73.2 %last_sums.1 = (f32[256,1024]{1,0:T(8,128)}, f32[8,1024]{1,0:T(8,128)}, f32[8,1024]{1,0:T(8,128)}, f32[128,2176]{1,0:T(8,128)}) custom-call(bf16[1024,1664]{1,0:T(8,128)(2,1)} %get-tuple-element.71.gproj_ref, bf16[2176,1024]{1,0:T(8,128)(2,1)} %all-gather.3.cloned.1.call-done.out_w_ref.w_ref, bf16[1024,1024]{1,0:T(8,128)(2,1)} %get-tuple-element.72.normed_ref, ...), custom_call_target="tpu_custom_call" | custom-call | bytes 165000000 | tf_op jit(solution)/shard_map/last_sums/pallas_call | solution.py:1110
  341.7 2.0 slice_bitcast_fusion.1
  343.6 0.8 copy.62
  344.5 1.0 fusion.30
  345.5 0.6 copy.60
  346.1 0.6 copy.61
  346.7 1.3 fusion.27
  348.0 0.8 constant_dynamic-slice_fusion.5
  348.8 1.3 dynamic-slice_bitcast_fusion
  350.1 1.3 constant_dynamic-slice_fusion
  351.4 1.3 constant_dynamic-slice_fusion.1
  352.8 0.6 slice_bitcast_fusion.4
  353.3 1.7 fusion.31
  355.0 1.2 convert_element_type.64
  356.3 0.9 copy.65
  357.3 0.9 copy.63
  358.2 0.9 copy.64
  359.1 1.0 copy.81
  (61 shorter events, 0.7 us)
Async XLA Ops:
  7.2 8.0 %copy-start.8 = (bf16[128,704]{0,1:T(8,128)(2,1)S(1)}, bf16[128,704]{0,1:T(8,128)(2,1)}, u32[]{:S(2)}) copy-start(bf16[128,704]{0,1:T(8,128)(2,1)} %param.38) | copy-start | bytes 540676
  7.2 8.0 %copy-start.7 = (bf16[128,704]{0,1:T(8,128)(2,1)S(1)}, bf16[128,704]{0,1:T(8,128)(2,1)}, u32[]{:S(2)}) copy-start(bf16[128,704]{0,1:T(8,128)(2,1)} %param.39) | copy-start | bytes 540676
  7.2 8.0 %copy-start.6 = (bf16[704,128]{1,0:T(8,128)(2,1)S(1)}, bf16[704,128]{1,0:T(8,128)(2,1)}, u32[]{:S(2)}) copy-start(bf16[704,128]{1,0:T(8,128)(2,1)} %param.40) | copy-start | bytes 540676
  7.2 9.6 %copy-start.11 = (bf16[32]{0:T(256)(128)(2,1)S(1)}, bf16[32]{0:T(256)(128)(2,1)}, u32[]{:S(2)}) copy-start(bf16[32]{0:T(256)(128)(2,1)} %param.23) | copy-start | bytes 196
  7.2 9.6 %copy-start.10 = (bf16[8]{0:T(256)(128)(2,1)S(1)}, bf16[8]{0:T(256)(128)(2,1)}, u32[]{:S(2)}) copy-start(bf16[8]{0:T(256)(128)(2,1)} %param.35) | copy-start | bytes 52
  7.2 9.6 %copy-start.9 = (bf16[32]{0:T(256)(128)(2,1)S(1)}, bf16[32]{0:T(256)(128)(2,1)}, u32[]{:S(2)}) copy-start(bf16[32]{0:T(256)(128)(2,1)} %param.37) | copy-start | bytes 196
  7.3 54.7 %all-gather.3.cloned.1.call-start = ((), (), s32[]{:S(2)}) async-start(), calls=%async_computation.2 | async-start | bytes 5013504 | tf_op jit(solution)/shard_map/all_gather | solution.py:1166
  11.4 48.9 %copy-start.14 = (bf16[2]{0:T(256)(128)(2,1)S(1)}, bf16[2]{0:T(256)(128)(2,1)}, u32[]{:S(2)}) copy-start(bf16[2]{0:T(256)(128)(2,1)} %param.33) | copy-start | bytes 16
  11.4 48.9 %copy-start.15 = (bf16[2]{0:T(256)(128)(2,1)S(1)}, bf16[2]{0:T(256)(128)(2,1)}, u32[]{:S(2)}) copy-start(bf16[2]{0:T(256)(128)(2,1)} %param.34) | copy-start | bytes 16
  11.5 49.6 %copy-start.3 = (bf16[256,1024]{1,0:T(8,128)(2,1)S(1)}, bf16[256,1024]{1,0:T(8,128)(2,1)}, u32[]{:S(2)}) copy-start(bf16[256,1024]{1,0:T(8,128)(2,1)} %param.41) | copy-start | bytes 1572868
  14.3 0.8 copy-start.5
  15.1 140.6 %all-gather.5.cloned.1.call-start = ((), (), s32[]{:S(2)}) async-start(), calls=%async_computation.3 | async-start | bytes 5308416 | tf_op jit(solution)/shard_map/all_gather | solution.py:1198
  16.1 249.2 %reduce-scatter.3.cloned.1.call-start = ((), (), s32[]{:S(2)}) async-start(), calls=%async_computation.4 | async-start | bytes 2621440 | tf_op jit(solution)/shard_map/reduce_scatter | solution.py:1210
  219.8 1.6 copy-start
  219.8 135.2 %reduce-scatter.5.cloned.1.call-start = ((), (), s32[]{:S(2)}) async-start(), calls=%async_computation.5 | async-start | bytes 5308416 | tf_op jit(solution)/shard_map/reduce_scatter | solution.py:1209
  221.3 3.4 copy-start.12
  221.3 3.4 copy-start.13
  231.4 34.0 %copy-start.2 = (bf16[256,1024]{1,0:T(8,128)(2,1)S(1)}, bf16[256,1024]{1,0:T(8,128)(2,1)}, u32[]{:S(2)}) copy-start(bf16[256,1024]{1,0:T(8,128)(2,1)} %x_ref) | copy-start | bytes 1572868
  355.0 2.2 copy-start.1
  356.3 2.8 copy-start.4
Sparse Core Ops, SparseCore 0:
  15.3 39.5 all-gather.2
  57.3 39.6 all-gather.4
  219.9 44.5 reduce-scatter.2
  267.8 70.0 reduce-scatter.4

commit v3 on v2

--- a/solution.py
+++ b/solution.py
@@ -103,7 +103,7 @@
     pl.semaphore_wait(barrier, jnp.where(me > 0, 1, 0) + jnp.where(me < size - 1, 1, 0))
 
 
-PIECE = 32
+PIECE = 64
 
 
 class StreamSum:
@@ -1022,7 +1022,7 @@
     done = groups * per
     for stage in range(stages):
         if stage > 0:
-            until = max(done, int(ticks * (0.68 + 0.24 * (stage - 1) / max(stages - 2, 1))))
+            until = max(done, int(ticks * (0.45 + 0.3 * (stage - 1) / max(stages - 2, 1))))
 
             @pl.loop(done, until)
             def _(t):

time: 368 us -> 362 us (0.984)
  Pallas kernels: 299 us -> 292 us
    pallas_call x1, Pallas kernels: 73.2 us -> 67.6 us  [last_sums(): pl.pallas_call(functools.partial(last_kernel, fsdp, size, pieces, slack),...]
  transfers between devices with their start and end apart: 4 -> 4, of which waited for: 0 -> 0; matrix products, arithmetic and copies ran while one was open for 10% -> 11% of each run, Pallas kernels for 64% -> 64%
where the time goes in v3:
time: 362 us; the launch traced here: 360 us
  Pallas kernels  292 us (81%)
  local copies, waits for them, and re-layouts  32 us (9%)
  between operations  14.8 us (4%)
  other arithmetic  13 us (4%)
  matrix products  7.45 us (2%)
    pallas_call x1, Pallas kernels, mixer_fwd(): pl.pallas_call(functools.partial(fwd_kernel, size, lag, heads, dk, dv), g...  90.8 us
    pallas_call x1, Pallas kernels, last_sums(): pl.pallas_call(functools.partial(last_kernel, fsdp, size, pieces, slack),...  67.6 us
    pallas_call x1, Pallas kernels, feed_forward(): pl.pallas_call(functools.partial(ff_kernel, size, lag, wide), grid=(chunk...  63.5 us
    pallas_call x1, Pallas kernels, line_gather(): pl.pallas_call(functools.partial(line_gather_kernel, fsdp, size, pieces),...  39.7 us
    pallas_call x1, Pallas kernels, mixer_bwd(): pl.pallas_call(functools.partial(bwd_kernel, heads, dk, dv), grid=(chunks...  30.9 us
    unnamed x50, local copies, waits for them, and re-layouts  12.9 us
  transfers between devices with their start and end apart: 4, of which 0 were waited for; matrix products, arithmetic and copies ran while one was open for 11% of the time, Pallas kernels for 64%

profile of v3, /device:TPU:12, one launch (start us, length us, event | category | flops | bytes accessed | tf_op | source)
XLA Modules:
  0.0 359.9 jit_solution(1080937855646866499)
XLA Ops:
  7.3 1.1 copy.52
  8.4 1.0 copy.53
  9.4 1.0 copy.54
  10.4 1.0 copy.55
  11.5 0.8 maximum_bitcast_fusion
  12.4 0.1 reshape.129
  12.4 0.1 copy.56
  12.7 0.7 fusion.9
  13.4 0.9 constant_dynamic-update-slice_fusion
  14.3 0.8 copy-done.5
  15.2 0.9 fusion.5
  16.8 0.7 fusion.26.tile_ref
  17.5 39.7 %line_gather.1 = (bf16[1024,1024]{1,0:T(8,128)(2,1)}, f32[8,4,8,128]{3,2,1,0:T(8,128)}) custom-call(bf16[256,1024]{1,0:T(8,128)(2,1)} %x_ref, f32[8,128]{1,0:T(8,128)} %fusion.26.tile_ref), custom_call_target="tpu_custom_call" | custom-call | bytes 120000000 | tf_op jit(solution)/shard_map/line_gather/pallas_call | solution.py:774
  57.2 0.9 slice.84
  58.1 0.1 slice.119
  58.3 0.7 broadcast_in_dim_reshape.7.norm_gain_ref.gain_ref
  58.9 0.1 tile.7
  59.0 0.6 copy.69
  59.6 0.7 broadcast_in_dim_reshape.8.gain_ref
  60.3 0.1 pad_bitcast_fusion
  60.4 0.1 bitcast_convert_fusion
  60.5 0.6 select_maximum_fusion.2.misc_ref
  61.1 0.9 broadcast_select_fusion.shard_ref
  62.0 1.0 slice.113
  63.0 0.2 copy.67
  63.2 0.1 reshape.132
  63.3 0.1 slice.118
  63.4 0.1 fusion.34
  63.5 0.1 reshape.134
  63.5 0.1 reshape.135
  63.6 0.1 reshape.136
  63.7 0.6 fusion.16.taps_ref
  64.3 90.8 %mixer_fwd.1 = (bf16[1024,1024]{1,0:T(8,128)(2,1)}, f32[1024,1664]{1,0:T(8,128)}, bf16[1024,512]{1,0:T(8,128)(2,1)}, f32[1024,512]{1,0:T(8,128)}, bf16[1024,512]...) custom-call(bf16[1024,1024]{1,0:T(8,128)(2,1)} %get-tuple-element.53, ...), custom_call_target="tpu_custom_call" | custom-call | bytes 264000000 | tf_op jit(solution)/shard_map/mixer_fwd/pallas_call | solution.py:389
  155.1 63.5 %feed_forward.1 = (bf16[1024,1024]{1,0:T(8,128)(2,1)}, bf16[1024,768]{1,0:T(8,128)(2,1)}, bf16[1024,1536]{1,0:T(8,128)(2,1)}, bf16[1024,1024]{1,0:T(8,128)(2,1)}...) custom-call(bf16[1024,1024]{1,0:T(8,128)(2,1)} %get-tuple-element.53.tokens_ref, f32[1024,1024]{1,0:T(8,128)} %get-tuple-element.56.branch_ref, ...), custom_call_target="tpu_custom_call" | custom-call | bytes 195000000 | tf_op jit(solution)/shard_map/feed_forward/pallas_call | solution.py:630
  218.7 1.5 copy-done
  220.2 3.4 convolution_convert_fusion.1
  223.7 4.0 %convolution_convert_fusion = bf16[1024,1536]{1,0:T(8,128)(2,1)S(1)} fusion(bf16[1024,1024]{1,0:T(8,128)(2,1)S(1)} %copy-done.13, bf16[1024,1536]{1,0:T(8,128)(2,1)S(1)} %copy-done.12), kind=kOutput, calls=%fused_computation.1 | convolution fusion | flops 3222798336 | bytes 8388608 | tf_op jit(solution)/shard_map/dot_general | solution.py:1205
  227.7 2.5 pad_maximum_fusion
  230.3 30.9 %mixer_bwd.1 = (bf16[1024,1024]{1,0:T(8,128)(2,1)}, bf16[1024,1664]{1,0:T(8,128)(2,1)}, f32[8,1024]{1,0:T(8,128)}, f32[8,128]{1,0:T(8,128)}, f32[8,512]{1,0:T(8,128)}) custom-call(bf16[1024,1024]{1,0:T(8,128)(2,1)} %get-tuple-element.57.grad_ref.out_grad_ref, f32[1024,1024]{1,0:T(8,128)} %get-tuple-element.63.sent_ref, ...), custom_call_target="tpu_custom_call" | custom-call | bytes 81000000 | tf_op jit(solution)/shard_map/mixer_bwd/pallas_call | solution.py:554
  261.1 0.7 slice_reduce_fusion
  261.9 0.8 slice.94
  262.7 0.8 slice_bitcast_fusion.7
  263.4 0.1 fusion.28
  263.5 0.1 select_bitcast_fusion
  263.6 0.6 select_maximum_fusion.small_ref
  264.2 3.1 dynamic-slice_add_fusion
  267.4 67.6 %last_sums.1 = (f32[256,1024]{1,0:T(8,128)}, f32[8,1024]{1,0:T(8,128)}, f32[8,1024]{1,0:T(8,128)}, f32[128,2176]{1,0:T(8,128)}) custom-call(bf16[1024,1664]{1,0:T(8,128)(2,1)} %get-tuple-element.71.gproj_ref, bf16[2176,1024]{1,0:T(8,128)(2,1)} %all-gather.3.cloned.1.call-done.out_w_ref.w_ref, bf16[1024,1024]{1,0:T(8,128)(2,1)} %get-tuple-element.72.normed_ref, ...), custom_call_target="tpu_custom_call" | custom-call | bytes 165000000 | tf_op jit(solution)/shard_map/last_sums/pallas_call | solution.py:1110
  335.0 2.0 slice_bitcast_fusion.1
  336.9 0.8 copy.62
  337.8 1.0 fusion.30
  338.8 0.6 copy.60
  339.4 0.6 copy.61
  340.0 1.3 fusion.27
  341.3 0.8 constant_dynamic-slice_fusion.5
  342.1 1.3 dynamic-slice_bitcast_fusion
  343.4 1.3 constant_dynamic-slice_fusion
  344.7 1.3 constant_dynamic-slice_fusion.1
  346.1 0.6 slice_bitcast_fusion.4
  346.6 1.7 fusion.31
  348.3 1.2 convert_element_type.64
  349.6 0.9 copy.65
  350.5 0.9 copy.63
  351.5 0.9 copy.64
  352.4 1.0 copy.81
  (61 shorter events, 0.7 us)
Async XLA Ops:
  7.2 8.0 %copy-start.8 = (bf16[128,704]{0,1:T(8,128)(2,1)S(1)}, bf16[128,704]{0,1:T(8,128)(2,1)}, u32[]{:S(2)}) copy-start(bf16[128,704]{0,1:T(8,128)(2,1)} %param.38) | copy-start | bytes 540676
  7.2 8.0 %copy-start.7 = (bf16[128,704]{0,1:T(8,128)(2,1)S(1)}, bf16[128,704]{0,1:T(8,128)(2,1)}, u32[]{:S(2)}) copy-start(bf16[128,704]{0,1:T(8,128)(2,1)} %param.39) | copy-start | bytes 540676
  7.2 8.0 %copy-start.6 = (bf16[704,128]{1,0:T(8,128)(2,1)S(1)}, bf16[704,128]{1,0:T(8,128)(2,1)}, u32[]{:S(2)}) copy-start(bf16[704,128]{1,0:T(8,128)(2,1)} %param.40) | copy-start | bytes 540676
  7.2 9.6 %copy-start.11 = (bf16[32]{0:T(256)(128)(2,1)S(1)}, bf16[32]{0:T(256)(128)(2,1)}, u32[]{:S(2)}) copy-start(bf16[32]{0:T(256)(128)(2,1)} %param.23) | copy-start | bytes 196
  7.2 9.6 %copy-start.10 = (bf16[8]{0:T(256)(128)(2,1)S(1)}, bf16[8]{0:T(256)(128)(2,1)}, u32[]{:S(2)}) copy-start(bf16[8]{0:T(256)(128)(2,1)} %param.35) | copy-start | bytes 52
  7.2 9.6 %copy-start.9 = (bf16[32]{0:T(256)(128)(2,1)S(1)}, bf16[32]{0:T(256)(128)(2,1)}, u32[]{:S(2)}) copy-start(bf16[32]{0:T(256)(128)(2,1)} %param.37) | copy-start | bytes 196
  7.3 54.7 %all-gather.3.cloned.1.call-start = ((), (), s32[]{:S(2)}) async-start(), calls=%async_computation.2 | async-start | bytes 5013504 | tf_op jit(solution)/shard_map/all_gather | solution.py:1166
  11.4 48.9 %copy-start.14 = (bf16[2]{0:T(256)(128)(2,1)S(1)}, bf16[2]{0:T(256)(128)(2,1)}, u32[]{:S(2)}) copy-start(bf16[2]{0:T(256)(128)(2,1)} %param.33) | copy-start | bytes 16
  11.4 48.9 %copy-start.15 = (bf16[2]{0:T(256)(128)(2,1)S(1)}, bf16[2]{0:T(256)(128)(2,1)}, u32[]{:S(2)}) copy-start(bf16[2]{0:T(256)(128)(2,1)} %param.34) | copy-start | bytes 16
  11.5 49.6 %copy-start.3 = (bf16[256,1024]{1,0:T(8,128)(2,1)S(1)}, bf16[256,1024]{1,0:T(8,128)(2,1)}, u32[]{:S(2)}) copy-start(bf16[256,1024]{1,0:T(8,128)(2,1)} %param.41) | copy-start | bytes 1572868
  14.3 0.8 copy-start.5
  15.1 140.0 %all-gather.5.cloned.1.call-start = ((), (), s32[]{:S(2)}) async-start(), calls=%async_computation.3 | async-start | bytes 5308416 | tf_op jit(solution)/shard_map/all_gather | solution.py:1198
  16.1 248.1 %reduce-scatter.3.cloned.1.call-start = ((), (), s32[]{:S(2)}) async-start(), calls=%async_computation.4 | async-start | bytes 2621440 | tf_op jit(solution)/shard_map/reduce_scatter | solution.py:1210
  218.6 1.6 copy-start
  218.7 129.7 %reduce-scatter.5.cloned.1.call-start = ((), (), s32[]{:S(2)}) async-start(), calls=%async_computation.5 | async-start | bytes 5308416 | tf_op jit(solution)/shard_map/reduce_scatter | solution.py:1209
  220.2 3.4 copy-start.12
  220.2 3.4 copy-start.13
  230.3 34.0 %copy-start.2 = (bf16[256,1024]{1,0:T(8,128)(2,1)S(1)}, bf16[256,1024]{1,0:T(8,128)(2,1)}, u32[]{:S(2)}) copy-start(bf16[256,1024]{1,0:T(8,128)(2,1)} %x_ref) | copy-start | bytes 1572868
  348.3 2.2 copy-start.1
  349.6 2.8 copy-start.4
Sparse Core Ops, SparseCore 0:
  15.3 39.5 all-gather.2
  57.3 39.6 all-gather.4
  218.8 44.1 reduce-scatter.2
  266.3 66.8 reduce-scatter.4
